TPU v7x, 128 devices: a whole 4x4x4 slice. The times are simulated.
128 devices in a mesh: sect: 2 (over core), tmpl: 64 (over z, y, x).
Axes of the slice: x: 4, y: 4, z: 4, core: 2. Of those that a mesh axis runs over, the one named last changes fastest.
Arguments:
- strain: bfloat16 [2, 1535], P('sect'), may hold values from -6 to 6
- filters: bfloat16 [2, 1024, 1024], P('sect', 'tmpl'), may hold values from -0.1875 to 0.1875
- synthesis: bfloat16 [2, 32768, 1024], P('sect', 'tmpl'), may hold values from -0.1875 to 0.1875
- correlation: float32 [16384, 2, 351], P('tmpl'), may hold values from -0.6 to 0.6
Outputs:
- snr: bfloat16 [32768, 512], P('tmpl', 'sect')
- residual: float32 [16384, 512], P('tmpl', 'sect')
All inputs are finite; a program needn't handle non-finite values.
Results may differ from a plain program's by a relative error of at most 0.0049.
Values may be sent and summed in bfloat16 or wider, within the bound.
No kernel may reach another device: no remote copies, remote signals or barrier semaphores. Data moves between devices by JAX's collectives and lax.ppermute only.
A program may use at most 64 MiB of HBM per device.

v0:
```python
import functools

import jax
import jax.numpy as jnp
import numpy as np
from jax import lax
from jax.experimental import pallas as pl
from jax.experimental.pallas import tpu as pltpu
from jax.sharding import PartitionSpec as P

KMAX = 4
PERIOD = 767
BINS = 384
LANES = 128


def forward_matrix(rows):
    angle = 2.0 * np.pi * np.outer(np.arange(rows), np.arange(BINS)) / PERIOD
    return np.concatenate([np.cos(angle), -np.sin(angle)], axis=1)


def inverse_matrix(samples, half):
    angle = 2.0 * np.pi * np.outer(np.arange(BINS), np.arange(samples) - half) / PERIOD
    share = np.where(np.arange(BINS) == 0, 0.5, 1.0)[:, None]
    return np.concatenate([share * np.cos(angle), -share * np.sin(angle)], axis=0)


def conv_kernel(strain_ref, filters_ref, basis_ref, line_ref):
    section = lax.axis_index("sect")
    taps = filters_ref.shape[1]
    samples = basis_ref.shape[1]
    width = line_ref.shape[1]
    rows = 256
    line_ref[...] = jnp.zeros_like(line_ref)
    line_ref[0:1, 0 : strain_ref.shape[1]] = strain_ref[...].astype(jnp.float32)
    spread = jnp.broadcast_to(line_ref[0:1, :], (rows, width))
    shifted = pltpu.roll(spread, width - (rows - 1), 1, stride=1, stride_axis=0).astype(jnp.bfloat16)
    row = lax.broadcasted_iota(jnp.int32, (rows, rows), 0)
    col = lax.broadcasted_iota(jnp.int32, (rows, rows), 1)
    flip = (row + col == rows - 1).astype(jnp.float32).astype(jnp.bfloat16)
    total = jnp.zeros((filters_ref.shape[0], samples), jnp.float32)
    for start in range(0, taps, rows):
        part = jnp.dot(filters_ref[:, start : start + rows], flip, preferred_element_type=jnp.float32)
        total += jnp.dot(
            part.astype(jnp.bfloat16), shifted[:, start : start + samples], preferred_element_type=jnp.float32
        )
    basis = total.astype(jnp.bfloat16)
    source = lax.broadcasted_iota(jnp.int32, (samples, samples), 0)
    target = lax.broadcasted_iota(jnp.int32, (samples, samples), 1)
    hold_log = lax.axis_size("sect") - 1 - section
    pick = (source == (target >> hold_log)).astype(jnp.float32).astype(jnp.bfloat16)
    basis_ref[...] = jnp.dot(basis, pick, preferred_element_type=jnp.float32).astype(jnp.bfloat16)


def held_basis(strain, filters, samples):
    width = strain.shape[1] + 1
    return pl.pallas_call(
        conv_kernel,
        out_shape=jax.ShapeDtypeStruct((filters.shape[0], samples), jnp.bfloat16),
        scratch_shapes=[pltpu.VMEM((8, width), jnp.float32)],
        name="held_basis",
    )(strain, filters)


def lags_kernel(series_ref, forward_ref, spectrum_ref, weight_ref):
    groups = weight_ref.shape[0]
    length = series_ref.shape[1]
    real_part = series_ref[0:groups, :]
    imag_part = series_ref[groups:, :]
    weight_ref[...] = jnp.sum(real_part * real_part + imag_part * imag_part, axis=1, keepdims=True)
    table = forward_ref[0:length, :]
    spectrum_ref[0:groups, :] = jnp.dot(real_part.astype(jnp.bfloat16), table, preferred_element_type=jnp.float32)
    spectrum_ref[groups:, :] = jnp.dot(imag_part.astype(jnp.bfloat16), table, preferred_element_type=jnp.float32)


def lag_spectrum(correlation, forward):
    groups, _, length = correlation.shape
    return pl.pallas_call(
        lags_kernel,
        out_shape=(
            jax.ShapeDtypeStruct((2 * groups, 2 * BINS), jnp.float32),
            jax.ShapeDtypeStruct((groups, 1), jnp.float32),
        ),
        name="lag_spectrum",
    )(jnp.swapaxes(correlation, 0, 1).reshape(2 * groups, length), forward)


def residual_kernel(half, own_ref, other_ref, spectrum_ref, weight_ref, forward_ref, inverse_ref, snr_ref, residual_ref, full_ref):
    section = lax.axis_index("sect")
    groups, share = residual_ref.shape
    samples = own_ref.shape[1]
    length = 2 * half + 1
    tiles = samples // LANES
    for tile in range(tiles):
        lanes = slice(tile * LANES, (tile + 1) * LANES)
        full_ref[tile] = own_ref[:, lanes] + other_ref[:, lanes]
    first = pl.multiple_of(section * share, share)
    mine = pl.ds(first, share)
    own_tiles = [section * (share // LANES) + step for step in range(share // LANES)]
    even = pl.ds(0, groups, stride=2)
    odd = pl.ds(1, groups, stride=2)

    def joined(rows, which):
        return jnp.concatenate([full_ref[tile, rows, :] for tile in which], axis=1)

    snr_ref[...] = joined(slice(None), own_tiles).astype(jnp.bfloat16)
    real_all = joined(even, range(tiles))
    imag_all = joined(odd, range(tiles))
    real_mid = joined(even, own_tiles)
    imag_mid = joined(odd, own_tiles)
    power = real_all * real_all + imag_all * imag_all
    high = power.astype(jnp.bfloat16)
    low = (power - high.astype(jnp.float32)).astype(jnp.bfloat16)
    source = lax.broadcasted_iota(jnp.int32, (samples, share), 0)
    target = lax.broadcasted_iota(jnp.int32, (samples, share), 1) + first
    band = (jnp.abs(source - target) <= half).astype(jnp.float32).astype(jnp.bfloat16)
    energy = jnp.dot(high, band, preferred_element_type=jnp.float32)
    energy += jnp.dot(low, band, preferred_element_type=jnp.float32)
    table = forward_ref[...]
    real_hat = jnp.dot(real_all.astype(jnp.bfloat16), table, preferred_element_type=jnp.float32)
    imag_hat = jnp.dot(imag_all.astype(jnp.bfloat16), table, preferred_element_type=jnp.float32)
    a_real, a_imag = real_hat[:, :BINS], real_hat[:, BINS:]
    b_real, b_imag = imag_hat[:, :BINS], imag_hat[:, BINS:]
    p_real, p_imag = spectrum_ref[0:groups, 0:BINS], spectrum_ref[0:groups, BINS:]
    q_real, q_imag = spectrum_ref[groups:, 0:BINS], spectrum_ref[groups:, BINS:]
    scale = jnp.float32(2.0 / PERIOD)
    back = inverse_ref[:, mine]

    def turned(low_part, high_part):
        parts = jnp.concatenate([low_part * scale, high_part * scale], axis=1).astype(jnp.bfloat16)
        return jnp.dot(parts, back, preferred_element_type=jnp.float32)

    real_sum = turned(
        a_real * p_real + a_imag * p_imag + b_real * q_real + b_imag * q_imag,
        a_imag * p_real - a_real * p_imag + b_imag * q_real - b_real * q_imag,
    )
    imag_sum = turned(
        b_real * p_real + b_imag * p_imag - a_real * q_real - a_imag * q_imag,
        b_imag * p_real - b_real * p_imag - a_imag * q_real + a_real * q_imag,
    )
    cross = real_mid * real_sum + imag_mid * imag_sum
    magnitude = real_mid * real_mid + imag_mid * imag_mid
    residual_ref[...] = (energy - 2.0 * cross + magnitude * weight_ref[...]) * jnp.float32(1.0 / (2.0 * length))


def residual_of(own, other, spectrum, weight, forward, inverse, half, share):
    columns = own.shape[0]
    return pl.pallas_call(
        functools.partial(residual_kernel, half),
        out_shape=(
            jax.ShapeDtypeStruct((columns, share), jnp.bfloat16),
            jax.ShapeDtypeStruct((columns // 2, share), jnp.float32),
        ),
        scratch_shapes=[pltpu.VMEM((own.shape[1] // LANES, columns, LANES), jnp.float32)],
        name="residual",
    )(own, other, spectrum, weight, forward, inverse)


def local(strain, filters, synthesis, correlation):
    sections = lax.axis_size("sect")
    chips = lax.axis_size("tmpl")
    taps = filters.shape[2]
    samples = strain.shape[1] - taps + 1
    share = samples // sections
    half = (correlation.shape[2] - 1) // 2
    forward = jnp.asarray(forward_matrix(samples), jnp.bfloat16)
    inverse = jnp.asarray(inverse_matrix(samples, half), jnp.bfloat16)
    basis = held_basis(strain, filters[0], samples)
    spectrum, weight = lag_spectrum(correlation, forward)
    block = jnp.broadcast_to(basis[None], (chips,) + basis.shape)
    piece = lax.all_to_all(block, "tmpl", 0, 0).reshape(-1, samples)
    own = jnp.dot(synthesis[0], piece, preferred_element_type=jnp.float32)
    other = lax.ppermute(own, "sect", [(0, 1), (1, 0)])
    return residual_of(own, other, spectrum, weight, forward, inverse, half, share)


def solution(mesh):
    placed = (
        P("sect", None),
        P("sect", "tmpl", None),
        P("sect", "tmpl", None),
        P("tmpl", None, None),
    )
    return jax.shard_map(
        local,
        mesh=mesh,
        in_specs=placed,
        out_specs=(P("tmpl", "sect"), P("tmpl", "sect")),
        check_vma=False,
    )
```

profile of v0, /device:TPU:1, one launch (start us, length us, event | category | flops | bytes accessed | tf_op | source)
XLA Modules:
  0.0 47.2 jit_solution(2932842436777737977)
XLA Ops:
  0.6 0.0 copy-start
  0.6 2.2 %held_basis.1 = bf16[16,512]{1,0:T(8,128)(2,1)} custom-call(bf16[1,1535]{1,0:T(2,128)(2,1)} %strain_ref.1, bf16[16,1024]{1,0:T(8,128)(2,1)} %bitcast.13), custom_call_target="tpu_custom_call" | custom-call | tf_op jit(solution)/shard_map/held_basis/pallas_call | solution.py:57
  2.9 0.8 %broadcast_in_dim.2 = bf16[64,16,512]{2,1,0:T(8,128)(2,1)S(1)} broadcast(bf16[16,512]{1,0:T(8,128)(2,1)} %held_basis.1), dimensions={1,2} | broadcast | bytes 1064960 | tf_op jit(solution)/shard_map/broadcast_in_dim | solution.py:170
  3.7 29.5 %all_to_all.5 = bf16[64,16,512]{2,1,0:T(8,128)(2,1)S(1)} all-to-all(bf16[64,16,512]{2,1,0:T(8,128)(2,1)S(1)} %broadcast_in_dim.2), channel_id=1, replica_groups=mesh['sect'=2,'tmpl'=64] {'tmpl'}, dimensions={0} | all-to-all | bytes 2097152 | tf_op jit(solution)/shard_map/all_to_all | solution.py:171
  33.2 0.0 copy-done
  33.2 0.7 %convolution_bitcast_fusion.own_ref = f32[512,512]{1,0:T(8,128)S(1)} fusion(bf16[1024,512]{1,0:T(8,128)(2,1)S(1)} %bitcast.11, bf16[1,512,1024]{2,1,0:T(8,128)(2,1)S(1)} %copy-done), kind=kOutput, calls=%fused_computation | convolution fusion | flops 536870912 | bytes 3145728 | tf_op jit(solution)/shard_map/dot_general | solution.py:172
  33.9 0.0 copy-start.1
  33.9 2.2 %collective-permute-start = (f32[512,512]{1,0:T(8,128)S(1)}, f32[512,512]{1,0:T(8,128)S(1)}, u32[]{:S(2)}, u32[]{:S(2)}) collective-permute-start(f32[512,512]{1,0:T(8,128)S(1)} %convolution_bitcast_fusion.own_ref), channel_id=1, source_target_pairs={{0,64},{64,0},{1,65},{65,1},{2,66},{66,2},{3,67},{67,3},{4,68},{68... | collective-permute-start | bytes 3145736 | tf_op jit(solution)/shard_map/ppermute | solution.py:173
  36.1 2.1 %copy.9 = f32[2,256,351]{2,1,0:T(8,128)} copy(f32[2,256,351]{1,0,2:T(2,128)} %bitcast.12) | data formatting | bytes 1437696 | tf_op jit(solution)/shard_map/transpose | solution.py:85
  38.2 3.1 %lag_spectrum.1 = (f32[512,768]{1,0:T(8,128)}, f32[256,1]{1,0:T(8,128)}) custom-call(f32[512,351]{1,0:T(8,128)} %bitcast.10, bf16[512,768]{1,0:T(8,128)(2,1)} %constant.4.clone.forward_ref), custom_call_target="tpu_custom_call" | custom-call | tf_op jit(solution)/shard_map/lag_spectrum/pallas_call | solution.py:78
  41.3 0.0 collective-permute-done.other_ref
  41.3 0.0 copy-start.2
  41.3 0.0 copy-done.1
  41.3 1.0 %copy-done.2 = f32[512,512]{1,0:T(8,128)} copy-done((f32[512,512]{1,0:T(8,128)}, f32[512,512]{1,0:T(8,128)S(1)}, u32[]{:S(2)}) %copy-start.2) | copy-done | bytes 1048600
  42.3 4.9 %residual.1 = (bf16[512,256]{1,0:T(8,128)(2,1)}, f32[256,256]{1,0:T(8,128)}) custom-call(f32[512,512]{1,0:T(8,128)} %copy-done.1, f32[512,512]{1,0:T(8,128)} %copy-done.2, f32[512,768]{1,0:T(8,128)} %get-tuple-element.4.spectrum_ref, f32[256,1]{1,0:T(8,128)} %get-tuple-element.5.weight_ref, bf16[512,768]{1,0:T(8,128)(2,1)} %constant.4.clone.forward_ref, ...), custom_call_target="tpu_custom_call" | custom-call | tf_op jit(solution)/shard_map/residual/pallas_call | solution.py:148
Async XLA Ops:
  0.6 32.6 %copy-start = (bf16[1,512,1024]{2,1,0:T(8,128)(2,1)S(1)}, bf16[1,512,1024]{2,1,0:T(8,128)(2,1)}, u32[]{:S(2)}) copy-start(bf16[1,512,1024]{2,1,0:T(8,128)(2,1)} %param.8) | copy-start | bytes 3145732
  33.9 7.4 %copy-start.1 = (f32[512,512]{1,0:T(8,128)}, f32[512,512]{1,0:T(8,128)S(1)}, u32[]{:S(2)}) copy-start(f32[512,512]{1,0:T(8,128)S(1)} %convolution_bitcast_fusion.own_ref) | copy-start | bytes 3145732
  33.9 7.4 %collective-permute-start = (f32[512,512]{1,0:T(8,128)S(1)}, f32[512,512]{1,0:T(8,128)S(1)}, u32[]{:S(2)}, u32[]{:S(2)}) collective-permute-start(f32[512,512]{1,0:T(8,128)S(1)} %convolution_bitcast_fusion.own_ref), channel_id=1, source_target_pairs={{0,64},{64,0},{1,65},{65,1},{2,66},{66,2},{3,67},{67,3},{4,68},{68... | collective-permute-start | bytes 3145736 | tf_op jit(solution)/shard_map/ppermute | solution.py:173
  41.3 1.0 %copy-start.2 = (f32[512,512]{1,0:T(8,128)}, f32[512,512]{1,0:T(8,128)S(1)}, u32[]{:S(2)}) copy-start(f32[512,512]{1,0:T(8,128)S(1)} %collective-permute-done.other_ref) | copy-start | bytes 3145732
where the time goes:
time: 47.5 us; the launch traced here: 47.2 us
  blocking collectives  29.5 us (62%)
  Pallas kernels  10.2 us (21%)
  local copies, waits for them, and re-layouts  3.91 us (8%)
  starting transfers between devices  2.2 us (5%)
  matrix products  0.7 us (1%)
  between operations  0.67 us (1%)
    all_to_all x1, blocking collectives, local(): piece = lax.all_to_all(block, 'tmpl', 0, 0).reshape(-1, samples)  29.5 us
    pallas_call x1, Pallas kernels, residual_of(): pl.pallas_call(functools.partial(residual_kernel, half), out_shape=(jax.S...  4.88 us
    pallas_call x1, Pallas kernels, lag_spectrum(): pl.pallas_call(lags_kernel, out_shape=(jax.ShapeDtypeStruct((2 * groups,...  3.14 us
    pallas_call x1, Pallas kernels, held_basis(): pl.pallas_call(conv_kernel, out_shape=jax.ShapeDtypeStruct((filters.shape...  2.22 us
    ppermute x1, starting transfers between devices, local(): other = lax.ppermute(own, 'sect', [(0, 1), (1, 0)])  2.2 us
    transpose x1, local copies, waits for them, and re-layouts, lag_spectrum(): jnp.swapaxes(correlation, 0, 1).reshape(2 * groups, length)  2.09 us
    unnamed x6, local copies, waits for them, and re-layouts  0.99 us
  transfers between devices with their start and end apart: 1, of which 0 were waited for; matrix products, arithmetic and copies ran while one was open for 4% of the time, Pallas kernels for 7%

commit v1 on v0

--- a/solution.py
+++ b/solution.py
@@ -12,6 +12,7 @@
 PERIOD = 767
 BINS = 384
 LANES = 128
+GRANT = 24 << 20
 
 
 def forward_matrix(rows):
@@ -28,7 +29,7 @@
 def conv_kernel(strain_ref, filters_ref, basis_ref, line_ref):
     section = lax.axis_index("sect")
     taps = filters_ref.shape[1]
-    samples = basis_ref.shape[1]
+    samples = basis_ref.shape[2]
     width = line_ref.shape[1]
     rows = 256
     line_ref[...] = jnp.zeros_like(line_ref)
@@ -49,40 +50,63 @@
     target = lax.broadcasted_iota(jnp.int32, (samples, samples), 1)
     hold_log = lax.axis_size("sect") - 1 - section
     pick = (source == (target >> hold_log)).astype(jnp.float32).astype(jnp.bfloat16)
-    basis_ref[...] = jnp.dot(basis, pick, preferred_element_type=jnp.float32).astype(jnp.bfloat16)
-
-
-def held_basis(strain, filters, samples):
+    held = jnp.dot(basis, pick, preferred_element_type=jnp.float32).astype(jnp.bfloat16)
+    for chip in range(basis_ref.shape[0]):
+        basis_ref[chip] = held
+
+
+def held_basis(strain, filters, samples, chips):
     width = strain.shape[1] + 1
     return pl.pallas_call(
         conv_kernel,
-        out_shape=jax.ShapeDtypeStruct((filters.shape[0], samples), jnp.bfloat16),
+        out_shape=jax.ShapeDtypeStruct((chips, filters.shape[0], samples), jnp.bfloat16),
         scratch_shapes=[pltpu.VMEM((8, width), jnp.float32)],
+        compiler_params=pltpu.CompilerParams(vmem_limit_bytes=GRANT),
         name="held_basis",
     )(strain, filters)
 
 
+def split(values):
+    high = values.astype(jnp.bfloat16)
+    return high, (values - high.astype(jnp.float32)).astype(jnp.bfloat16)
+
+
+def rows_dot(left, right):
+    return lax.dot_general(left, right, (((0,), (0,)), ((), ())), preferred_element_type=jnp.float32)
+
+
 def lags_kernel(series_ref, forward_ref, spectrum_ref, weight_ref):
+    length, pieces, lanes = series_ref.shape
     groups = weight_ref.shape[0]
-    length = series_ref.shape[1]
-    real_part = series_ref[0:groups, :]
-    imag_part = series_ref[groups:, :]
-    weight_ref[...] = jnp.sum(real_part * real_part + imag_part * imag_part, axis=1, keepdims=True)
+    flat = series_ref.reshape(length * pieces, lanes)
+
+    def part(which):
+        halves = [flat[pl.ds(2 * tile + which, length, stride=pieces), :] for tile in range(pieces // 2)]
+        return jnp.concatenate(halves, axis=1)
+
+    real_part, imag_part = part(0), part(1)
+    high, low = split(real_part * real_part + imag_part * imag_part)
+    ones = jnp.ones((length, lanes), jnp.bfloat16)
+    weight_ref[...] = rows_dot(high, ones) + rows_dot(low, ones)
     table = forward_ref[0:length, :]
-    spectrum_ref[0:groups, :] = jnp.dot(real_part.astype(jnp.bfloat16), table, preferred_element_type=jnp.float32)
-    spectrum_ref[groups:, :] = jnp.dot(imag_part.astype(jnp.bfloat16), table, preferred_element_type=jnp.float32)
+    spectrum_ref[0:groups, :] = rows_dot(real_part.astype(jnp.bfloat16), table)
+    spectrum_ref[groups:, :] = rows_dot(imag_part.astype(jnp.bfloat16), table)
 
 
 def lag_spectrum(correlation, forward):
     groups, _, length = correlation.shape
+    tiles = groups // LANES
+    series = correlation.transpose(2, 1, 0).reshape(length, 2, tiles, LANES)
+    series = series.transpose(0, 2, 1, 3).reshape(length, 2 * tiles, LANES)
     return pl.pallas_call(
         lags_kernel,
         out_shape=(
             jax.ShapeDtypeStruct((2 * groups, 2 * BINS), jnp.float32),
-            jax.ShapeDtypeStruct((groups, 1), jnp.float32),
+            jax.ShapeDtypeStruct((groups, LANES), jnp.float32),
         ),
+        compiler_params=pltpu.CompilerParams(vmem_limit_bytes=GRANT),
         name="lag_spectrum",
-    )(jnp.swapaxes(correlation, 0, 1).reshape(2 * groups, length), forward)
+    )(series, forward)
 
 
 def residual_kernel(half, own_ref, other_ref, spectrum_ref, weight_ref, forward_ref, inverse_ref, snr_ref, residual_ref, full_ref):
@@ -109,8 +133,7 @@
     real_mid = joined(even, own_tiles)
     imag_mid = joined(odd, own_tiles)
     power = real_all * real_all + imag_all * imag_all
-    high = power.astype(jnp.bfloat16)
-    low = (power - high.astype(jnp.float32)).astype(jnp.bfloat16)
+    high, low = split(power)
     source = lax.broadcasted_iota(jnp.int32, (samples, share), 0)
     target = lax.broadcasted_iota(jnp.int32, (samples, share), 1) + first
     band = (jnp.abs(source - target) <= half).astype(jnp.float32).astype(jnp.bfloat16)
@@ -140,7 +163,8 @@
     )
     cross = real_mid * real_sum + imag_mid * imag_sum
     magnitude = real_mid * real_mid + imag_mid * imag_mid
-    residual_ref[...] = (energy - 2.0 * cross + magnitude * weight_ref[...]) * jnp.float32(1.0 / (2.0 * length))
+    weight = jnp.concatenate([weight_ref[...]] * (share // LANES), axis=1)
+    residual_ref[...] = (energy - 2.0 * cross + magnitude * weight) * jnp.float32(1.0 / (2.0 * length))
 
 
 def residual_of(own, other, spectrum, weight, forward, inverse, half, share):
@@ -152,6 +176,7 @@
             jax.ShapeDtypeStruct((columns // 2, share), jnp.float32),
         ),
         scratch_shapes=[pltpu.VMEM((own.shape[1] // LANES, columns, LANES), jnp.float32)],
+        compiler_params=pltpu.CompilerParams(vmem_limit_bytes=GRANT),
         name="residual",
     )(own, other, spectrum, weight, forward, inverse)
 
@@ -165,9 +190,8 @@
     half = (correlation.shape[2] - 1) // 2
     forward = jnp.asarray(forward_matrix(samples), jnp.bfloat16)
     inverse = jnp.asarray(inverse_matrix(samples, half), jnp.bfloat16)
-    basis = held_basis(strain, filters[0], samples)
+    block = held_basis(strain, filters[0], samples, chips)
     spectrum, weight = lag_spectrum(correlation, forward)
-    block = jnp.broadcast_to(basis[None], (chips,) + basis.shape)
     piece = lax.all_to_all(block, "tmpl", 0, 0).reshape(-1, samples)
     own = jnp.dot(synthesis[0], piece, preferred_element_type=jnp.float32)
     other = lax.ppermute(own, "sect", [(0, 1), (1, 0)])

time: 47.5 us -> 40.3 us (0.85)
  Pallas kernels: 10.2 us -> 3.97 us
  local copies, waits for them, and re-layouts: 3.91 us -> 1.55 us
  waiting for transfers between devices: 0.01 us -> 1.55 us
    pallas_call x1, Pallas kernels: 4.88 us -> 2.37 us  [residual_of(): pl.pallas_call(functools.partial(residual_kernel, half), out_shape=(jax.S...]
    pallas_call x1, Pallas kernels: 3.14 us -> 0.73 us  [lag_spectrum(): pl.pallas_call(lags_kernel, out_shape=(jax.ShapeDtypeStruct((2 * groups,...]
    transpose x1 -> x0, local copies, waits for them, and re-layouts: 2.09 us -> none  [lag_spectrum(): jnp.swapaxes(correlation, 0, 1).reshape(2 * groups, length)]
    ppermute x1, waiting for transfers between devices: 0.01 us -> 1.55 us  [local(): other = lax.ppermute(own, 'sect', [(0, 1), (1, 0)])]
    pallas_call x1, Pallas kernels: 2.22 us -> 0.87 us  [held_basis(): pl.pallas_call(conv_kernel, out_shape=jax.ShapeDtypeStruct((chips, filter...]
    broadcast_in_dim x1 -> x0, local copies, waits for them, and re-layouts: 0.83 us -> none  [local(): block = jnp.broadcast_to(basis[None], (chips,) + basis.shape)]
    unnamed x6 -> x12, local copies, waits for them, and re-layouts: 0.99 us -> 1.55 us
  transfers between devices with their start and end apart: 1 -> 1, of which waited for: 0 -> 1; matrix products, arithmetic and copies ran while one was open for 4% -> 0% of each run, Pallas kernels for 7% -> 2%
where the time goes in v1:
time: 40.3 us; the launch traced here: 40.1 us
  blocking collectives  29.5 us (73%)
  Pallas kernels  3.97 us (10%)
  starting transfers between devices  2.2 us (5%)
  local copies, waits for them, and re-layouts  1.55 us (4%)
  waiting for transfers between devices  1.55 us (4%)
  matrix products  0.7 us (2%)
  between operations  0.68 us (2%)
    all_to_all x1, blocking collectives, local(): piece = lax.all_to_all(block, 'tmpl', 0, 0).reshape(-1, samples)  29.5 us
    pallas_call x1, Pallas kernels, residual_of(): pl.pallas_call(functools.partial(residual_kernel, half), out_shape=(jax.S...  2.37 us
    ppermute x1, starting transfers between devices, local(): other = lax.ppermute(own, 'sect', [(0, 1), (1, 0)])  2.2 us
    unnamed x12, local copies, waits for them, and re-layouts  1.55 us
    ppermute x1, waiting for transfers between devices, local(): other = lax.ppermute(own, 'sect', [(0, 1), (1, 0)])  1.55 us
    pallas_call x1, Pallas kernels, held_basis(): pl.pallas_call(conv_kernel, out_shape=jax.ShapeDtypeStruct((chips, filter...  0.87 us
  transfers between devices with their start and end apart: 1, of which 1 were waited for; matrix products, arithmetic and copies ran while one was open for 0% of the time, Pallas kernels for 2%

profile of v1, /device:TPU:1, one launch (start us, length us, event | category | flops | bytes accessed | tf_op | source)
XLA Modules:
  0.0 40.1 jit_solution(3901084791053710521)
XLA Ops:
  0.6 0.0 copy-start
  0.6 0.0 copy-start.4
  0.7 0.8 %copy-done.4 = bf16[1,16,1024]{2,1,0:T(8,128)(2,1)S(1)} copy-done((bf16[1,16,1024]{2,1,0:T(8,128)(2,1)S(1)}, bf16[1,16,1024]{2,1,0:T(8,128)(2,1)}, u32[]{:S(2)}) %copy-start.4) | copy-done | bytes 32792
  1.5 0.0 copy-start.5
  1.5 0.7 %copy-done.5 = bf16[1,1535]{1,0:T(2,128)(2,1)S(1)} copy-done((bf16[1,1535]{1,0:T(2,128)(2,1)S(1)}, bf16[1,1535]{1,0:T(2,128)(2,1)}, u32[]{:S(2)}) %copy-start.5) | copy-done | bytes 3094
  2.2 0.9 %held_basis.1 = bf16[64,16,512]{2,1,0:T(8,128)(2,1)S(1)} custom-call(bf16[1,1535]{1,0:T(2,128)(2,1)S(1)} %copy-done.5, bf16[16,1024]{1,0:T(8,128)(2,1)S(1)} %bitcast.16), custom_call_target="tpu_custom_call" | custom-call | tf_op jit(solution)/shard_map/held_basis/pallas_call | solution.py:60
  3.1 29.5 %all_to_all.5 = bf16[64,16,512]{2,1,0:T(8,128)(2,1)S(1)} all-to-all(bf16[64,16,512]{2,1,0:T(8,128)(2,1)S(1)} %held_basis.1), channel_id=1, replica_groups=mesh['sect'=2,'tmpl'=64] {'tmpl'}, dimensions={0} | all-to-all | bytes 2097152 | tf_op jit(solution)/shard_map/all_to_all | solution.py:195
  32.5 0.0 copy-done
  32.5 0.0 copy-start.1
  32.5 0.0 copy-start.3
  32.5 0.7 %convolution_bitcast_fusion.own_ref = f32[512,512]{1,0:T(8,128)S(1)} fusion(bf16[1024,512]{1,0:T(8,128)(2,1)S(1)} %bitcast.17, bf16[1,512,1024]{2,1,0:T(8,128)(2,1)S(1)} %copy-done), kind=kOutput, calls=%fused_computation | convolution fusion | flops 536870912 | bytes 3145728 | tf_op jit(solution)/shard_map/dot_general | solution.py:196
  33.3 0.0 copy-start.2
  33.3 2.2 %collective-permute-start = (f32[512,512]{1,0:T(8,128)S(1)}, f32[512,512]{1,0:T(8,128)S(1)}, u32[]{:S(2)}, u32[]{:S(2)}) collective-permute-start(f32[512,512]{1,0:T(8,128)S(1)} %convolution_bitcast_fusion.own_ref), channel_id=1, source_target_pairs={{0,64},{64,0},{1,65},{65,1},{2,66},{66,2},{3,67},{67,3},{4,68},{68... | collective-permute-start | bytes 3145736 | tf_op jit(solution)/shard_map/ppermute | solution.py:197
  35.5 0.0 copy-done.1
  35.5 0.0 copy-done.3
  35.5 0.7 %lag_spectrum.1 = (f32[512,768]{1,0:T(8,128)S(1)}, f32[256,128]{1,0:T(8,128)S(1)}) custom-call(f32[351,4,128]{2,1,0:T(4,128)S(1)} %bitcast.15, bf16[512,768]{1,0:T(8,128)(2,1)S(1)} %copy-done.1), custom_call_target="tpu_custom_call" | custom-call | tf_op jit(solution)/shard_map/lag_spectrum/pallas_call | solution.py:101
  36.2 1.5 %collective-permute-done.other_ref = f32[512,512]{1,0:T(8,128)S(1)} collective-permute-done((f32[512,512]{1,0:T(8,128)S(1)}, f32[512,512]{1,0:T(8,128)S(1)}, u32[]{:S(2)}, u32[]{:S(2)}) %collective-permute-start) | collective-permute-done | bytes 1048608 | tf_op jit(solution)/shard_map/ppermute | solution.py:197
  37.8 0.0 copy-done.2
  37.8 2.4 %residual.1 = (bf16[512,256]{1,0:T(8,128)(2,1)}, f32[256,256]{1,0:T(8,128)}) custom-call(f32[512,512]{1,0:T(8,128)S(1)} %convolution_bitcast_fusion.own_ref, f32[512,512]{1,0:T(8,128)S(1)} %collective-permute-done.other_ref, f32[512,768]{1,0:T(8,128)S(1)} %get-tuple-element.4.spectrum_ref, f32[256,128]{1,0:T(8,128)S(1)} %get-tuple-element.5.weight_ref, ...), custom_call_target="tpu_custom_call" | custom-call | tf_op jit(solution)/shard_map/residual/pallas_call | solution.py:172
Async XLA Ops:
  0.6 31.9 %copy-start = (bf16[1,512,1024]{2,1,0:T(8,128)(2,1)S(1)}, bf16[1,512,1024]{2,1,0:T(8,128)(2,1)}, u32[]{:S(2)}) copy-start(bf16[1,512,1024]{2,1,0:T(8,128)(2,1)} %param.8) | copy-start | bytes 3145732
  0.6 0.8 %copy-start.4 = (bf16[1,16,1024]{2,1,0:T(8,128)(2,1)S(1)}, bf16[1,16,1024]{2,1,0:T(8,128)(2,1)}, u32[]{:S(2)}) copy-start(bf16[1,16,1024]{2,1,0:T(8,128)(2,1)} %param.7) | copy-start | bytes 98308
  1.5 0.7 %copy-start.5 = (bf16[1,1535]{1,0:T(2,128)(2,1)S(1)}, bf16[1,1535]{1,0:T(2,128)(2,1)}, u32[]{:S(2)}) copy-start(bf16[1,1535]{1,0:T(2,128)(2,1)} %strain_ref.1) | copy-start | bytes 9214
  32.5 2.9 %copy-start.1 = (bf16[512,768]{1,0:T(8,128)(2,1)S(1)}, bf16[512,768]{1,0:T(8,128)(2,1)}, u32[]{:S(2)}) copy-start(bf16[512,768]{1,0:T(8,128)(2,1)} %constant.4.clone.forward_ref) | copy-start | bytes 2359300
  32.5 2.9 %copy-start.3 = (f32[256,2,351]{0,1,2:T(2,128)S(1)}, f32[256,2,351]{0,1,2:T(2,128)}, u32[]{:S(2)}) copy-start(f32[256,2,351]{0,1,2:T(2,128)} %param.9) | copy-start | bytes 2156548
  33.3 4.5 %copy-start.2 = (bf16[768,512]{1,0:T(8,128)(2,1)S(1)}, bf16[768,512]{1,0:T(8,128)(2,1)}, u32[]{:S(2)}) copy-start(bf16[768,512]{1,0:T(8,128)(2,1)} %constant.5.clone.inverse_ref) | copy-start | bytes 2359300
  33.3 4.5 %collective-permute-start = (f32[512,512]{1,0:T(8,128)S(1)}, f32[512,512]{1,0:T(8,128)S(1)}, u32[]{:S(2)}, u32[]{:S(2)}) collective-permute-start(f32[512,512]{1,0:T(8,128)S(1)} %convolution_bitcast_fusion.own_ref), channel_id=1, source_target_pairs={{0,64},{64,0},{1,65},{65,1},{2,66},{66,2},{3,67},{67,3},{4,68},{68... | collective-permute-start | bytes 3145736 | tf_op jit(solution)/shard_map/ppermute | solution.py:197

commit v2 on v1

--- a/solution.py
+++ b/solution.py
@@ -8,7 +8,7 @@
 from jax.experimental.pallas import tpu as pltpu
 from jax.sharding import PartitionSpec as P
 
-KMAX = 4
+
 PERIOD = 767
 BINS = 384
 LANES = 128
@@ -26,44 +26,86 @@
     return np.concatenate([share * np.cos(angle), -share * np.sin(angle)], axis=0)
 
 
-def conv_kernel(strain_ref, filters_ref, basis_ref, line_ref):
-    section = lax.axis_index("sect")
-    taps = filters_ref.shape[1]
-    samples = basis_ref.shape[2]
-    width = line_ref.shape[1]
+def convolved(line, bank, count):
     rows = 256
-    line_ref[...] = jnp.zeros_like(line_ref)
-    line_ref[0:1, 0 : strain_ref.shape[1]] = strain_ref[...].astype(jnp.float32)
-    spread = jnp.broadcast_to(line_ref[0:1, :], (rows, width))
-    shifted = pltpu.roll(spread, width - (rows - 1), 1, stride=1, stride_axis=0).astype(jnp.bfloat16)
+    taps = bank.shape[1]
+    width = line.shape[1]
     row = lax.broadcasted_iota(jnp.int32, (rows, rows), 0)
     col = lax.broadcasted_iota(jnp.int32, (rows, rows), 1)
     flip = (row + col == rows - 1).astype(jnp.float32).astype(jnp.bfloat16)
-    total = jnp.zeros((filters_ref.shape[0], samples), jnp.float32)
+    spread = jnp.broadcast_to(line, (rows, width))
+    shifted = pltpu.roll(spread, width - (rows - 1), 1, stride=1, stride_axis=0).astype(jnp.bfloat16)
+    total = jnp.zeros((bank.shape[0], count), jnp.float32)
     for start in range(0, taps, rows):
-        part = jnp.dot(filters_ref[:, start : start + rows], flip, preferred_element_type=jnp.float32)
+        part = jnp.dot(bank[:, start : start + rows], flip, preferred_element_type=jnp.float32)
         total += jnp.dot(
-            part.astype(jnp.bfloat16), shifted[:, start : start + samples], preferred_element_type=jnp.float32
+            part.astype(jnp.bfloat16), shifted[:, start : start + count], preferred_element_type=jnp.float32
         )
-    basis = total.astype(jnp.bfloat16)
-    source = lax.broadcasted_iota(jnp.int32, (samples, samples), 0)
-    target = lax.broadcasted_iota(jnp.int32, (samples, samples), 1)
-    hold_log = lax.axis_size("sect") - 1 - section
-    pick = (source == (target >> hold_log)).astype(jnp.float32).astype(jnp.bfloat16)
-    held = jnp.dot(basis, pick, preferred_element_type=jnp.float32).astype(jnp.bfloat16)
+    return total.astype(jnp.bfloat16)
+
+
+def first_kernel(line_hbm, bank_hbm, basis_ref, raw_ref, bank_ref, line_ref, sems):
+    section = lax.axis_index("sect")
+    taps = bank_ref.shape[1]
+    wide = basis_ref.shape[1]
+    line_copy = pltpu.make_async_copy(line_hbm, raw_ref, sems.at[0])
+    bank_copy = pltpu.make_async_copy(bank_hbm, bank_ref, sems.at[1])
+    line_copy.start()
+    bank_copy.start()
+    line_copy.wait()
+    line_ref[...] = jnp.zeros_like(line_ref)
+    line_ref[0:1, 0 : raw_ref.shape[1]] = raw_ref[...].astype(jnp.float32)
+    begin = pl.multiple_of(section * LANES, LANES)
+    line = line_ref[0:1, pl.ds(begin, taps + wide)]
+    bank_copy.wait()
+    basis_ref[...] = convolved(line, bank_ref[...], wide)
+
+
+def first_columns(line, bank, wide):
+    width = line.shape[1] + 1
+    return pl.pallas_call(
+        first_kernel,
+        in_specs=[pl.BlockSpec(memory_space=pltpu.HBM)] * 2,
+        out_shape=jax.ShapeDtypeStruct((bank.shape[0], wide), jnp.bfloat16),
+        scratch_shapes=[
+            pltpu.VMEM(line.shape, line.dtype),
+            pltpu.VMEM(bank.shape, bank.dtype),
+            pltpu.VMEM((8, width), jnp.float32),
+            pltpu.SemaphoreType.DMA((2,)),
+        ],
+        compiler_params=pltpu.CompilerParams(vmem_limit_bytes=GRANT),
+        cost_estimate=pl.CostEstimate(flops=1 << 30, bytes_accessed=1 << 22, transcendentals=0),
+        name="first_columns",
+    )(line, bank)
+
+
+def last_kernel(own_line_ref, other_line_ref, own_ref, other_ref, first_ref, basis_ref, line_ref):
+    section = lax.axis_index("sect")
+    taps = own_ref.shape[1]
+    share = basis_ref.shape[2]
+    length = own_line_ref.shape[1]
+    line_ref[...] = jnp.zeros_like(line_ref)
+    line_ref[0:1, 0:length] = own_line_ref[...].astype(jnp.float32)
+    line_ref[8:9, 0:length] = other_line_ref[...].astype(jnp.float32)
+    own = line_ref[0:1, share : share + taps + LANES]
+    line = jnp.where(section == 0, line_ref[8:9, 0 : taps + LANES], own)
+    bank = jnp.where(section == 0, other_ref[...].astype(jnp.float32), own_ref[...].astype(jnp.float32))
+    last = convolved(line, bank.astype(jnp.bfloat16), LANES)
+    basis = jnp.concatenate([first_ref[...], last], axis=1)
     for chip in range(basis_ref.shape[0]):
-        basis_ref[chip] = held
-
-
-def held_basis(strain, filters, samples, chips):
-    width = strain.shape[1] + 1
-    return pl.pallas_call(
-        conv_kernel,
-        out_shape=jax.ShapeDtypeStruct((chips, filters.shape[0], samples), jnp.bfloat16),
-        scratch_shapes=[pltpu.VMEM((8, width), jnp.float32)],
-        compiler_params=pltpu.CompilerParams(vmem_limit_bytes=GRANT),
-        name="held_basis",
-    )(strain, filters)
+        basis_ref[chip] = basis
+
+
+def basis_share(own_line, other_line, own, other, first, chips):
+    width = own_line.shape[1] + 1
+    share = first.shape[1] + LANES
+    return pl.pallas_call(
+        last_kernel,
+        out_shape=jax.ShapeDtypeStruct((chips, own.shape[0], share), jnp.bfloat16),
+        scratch_shapes=[pltpu.VMEM((16, width), jnp.float32)],
+        compiler_params=pltpu.CompilerParams(vmem_limit_bytes=GRANT),
+        name="basis_share",
+    )(own_line, other_line, own, other, first)
 
 
 def split(values):
@@ -73,6 +115,20 @@
 
 def rows_dot(left, right):
     return lax.dot_general(left, right, (((0,), (0,)), ((), ())), preferred_element_type=jnp.float32)
+
+
+def products(rows_ref, fast_own_ref, fast_other_ref, basis_ref, out_ref):
+    section = lax.axis_index("sect")
+    wide = basis_ref.shape[1] - LANES
+    out_ref[:, 0:wide] = jnp.dot(rows_ref[...], basis_ref[:, 0:wide], preferred_element_type=jnp.float32)
+
+    @pl.when(section == 0)
+    def _():
+        out_ref[:, wide:] = jnp.dot(fast_other_ref[...], basis_ref[:, wide:], preferred_element_type=jnp.float32)
+
+    @pl.when(section == 1)
+    def _():
+        out_ref[:, wide:] = jnp.dot(fast_own_ref[...], basis_ref[:, wide:], preferred_element_type=jnp.float32)
 
 
 def lags_kernel(series_ref, forward_ref, spectrum_ref, weight_ref):
@@ -105,19 +161,70 @@
             jax.ShapeDtypeStruct((groups, LANES), jnp.float32),
         ),
         compiler_params=pltpu.CompilerParams(vmem_limit_bytes=GRANT),
+        cost_estimate=pl.CostEstimate(flops=1 << 30, bytes_accessed=1 << 22, transcendentals=0),
         name="lag_spectrum",
     )(series, forward)
 
 
-def residual_kernel(half, own_ref, other_ref, spectrum_ref, weight_ref, forward_ref, inverse_ref, snr_ref, residual_ref, full_ref):
+def share_products(own, other, basis):
+    columns = own.shape[0]
+    share = basis.shape[1]
+    return pl.pallas_call(
+        lambda own_ref, other_ref, basis_ref, out_ref: products(own_ref, own_ref, other_ref, basis_ref, out_ref),
+        out_shape=jax.ShapeDtypeStruct((columns, share), jnp.float32),
+        compiler_params=pltpu.CompilerParams(vmem_limit_bytes=GRANT),
+        cost_estimate=pl.CostEstimate(flops=1 << 30, bytes_accessed=1 << 22, transcendentals=0),
+        name="share_products",
+    )(own, other, basis)
+
+
+def residual_kernel(
+    half,
+    own_ref,
+    other_ref,
+    basis_ref,
+    part_ref,
+    spectrum_ref,
+    weight_ref,
+    forward_ref,
+    inverse_ref,
+    snr_ref,
+    residual_ref,
+    full_ref,
+    rest_ref,
+    slow_ref,
+):
     section = lax.axis_index("sect")
     groups, share = residual_ref.shape
-    samples = own_ref.shape[1]
+    samples = forward_ref.shape[0]
     length = 2 * half + 1
     tiles = samples // LANES
+    wide = basis_ref.shape[1] - LANES
+    products(other_ref, own_ref, other_ref, basis_ref, rest_ref)
+
+    def placed(slow, middle, left, right):
+        slow_ref[...] = slow[:, 0:wide]
+        full_ref[0] = left[:, wide:]
+        for tile in range(1, tiles - 1):
+            full_ref[tile] = middle[:, (tile - 1) * LANES : tile * LANES]
+        full_ref[tiles - 1] = right[:, wide:]
+
+    @pl.when(section == 0)
+    def _():
+        placed(part_ref, rest_ref, part_ref, rest_ref)
+
+    @pl.when(section == 1)
+    def _():
+        placed(rest_ref, part_ref, rest_ref, part_ref)
+
+    source = lax.broadcasted_iota(jnp.int32, (wide, samples), 0)
+    target = lax.broadcasted_iota(jnp.int32, (wide, samples), 1)
+    hold = (source == target // 2).astype(jnp.float32).astype(jnp.bfloat16)
+    high, low = split(slow_ref[...])
+    held = jnp.dot(high, hold, preferred_element_type=jnp.float32)
+    held += jnp.dot(low, hold, preferred_element_type=jnp.float32)
     for tile in range(tiles):
-        lanes = slice(tile * LANES, (tile + 1) * LANES)
-        full_ref[tile] = own_ref[:, lanes] + other_ref[:, lanes]
+        full_ref[tile] += held[:, tile * LANES : (tile + 1) * LANES]
     first = pl.multiple_of(section * share, share)
     mine = pl.ds(first, share)
     own_tiles = [section * (share // LANES) + step for step in range(share // LANES)]
@@ -167,18 +274,23 @@
     residual_ref[...] = (energy - 2.0 * cross + magnitude * weight) * jnp.float32(1.0 / (2.0 * length))
 
 
-def residual_of(own, other, spectrum, weight, forward, inverse, half, share):
+def residual_of(own, other, basis, part, spectrum, weight, forward, inverse, half, share):
     columns = own.shape[0]
+    wide = basis.shape[1] - LANES
     return pl.pallas_call(
         functools.partial(residual_kernel, half),
         out_shape=(
             jax.ShapeDtypeStruct((columns, share), jnp.bfloat16),
             jax.ShapeDtypeStruct((columns // 2, share), jnp.float32),
         ),
-        scratch_shapes=[pltpu.VMEM((own.shape[1] // LANES, columns, LANES), jnp.float32)],
+        scratch_shapes=[
+            pltpu.VMEM((forward.shape[0] // LANES, columns, LANES), jnp.float32),
+            pltpu.VMEM(part.shape, jnp.float32),
+            pltpu.VMEM((columns, wide), jnp.float32),
+        ],
         compiler_params=pltpu.CompilerParams(vmem_limit_bytes=GRANT),
         name="residual",
-    )(own, other, spectrum, weight, forward, inverse)
+    )(own, other, basis, part, spectrum, weight, forward, inverse)
 
 
 def local(strain, filters, synthesis, correlation):
@@ -186,16 +298,25 @@
     chips = lax.axis_size("tmpl")
     taps = filters.shape[2]
     samples = strain.shape[1] - taps + 1
-    share = samples // sections
     half = (correlation.shape[2] - 1) // 2
+    share = (samples + samples // 2) // sections
+    swap = [(0, 1), (1, 0)]
     forward = jnp.asarray(forward_matrix(samples), jnp.bfloat16)
     inverse = jnp.asarray(inverse_matrix(samples, half), jnp.bfloat16)
-    block = held_basis(strain, filters[0], samples, chips)
+    own_bank = filters[0]
+    own_rows = synthesis[0]
+    other_line = lax.ppermute(strain, "sect", swap)
+    other_bank = lax.ppermute(own_bank, "sect", swap)
+    other_rows = lax.ppermute(own_rows, "sect", swap)
+    first = first_columns(strain, own_bank, share - LANES)
+    block = basis_share(strain, other_line, own_bank, other_bank, first, chips)
+    mine = lax.all_to_all(block, "tmpl", 0, 0).reshape(-1, share)
+    theirs = lax.ppermute(mine, "sect", swap)
     spectrum, weight = lag_spectrum(correlation, forward)
-    piece = lax.all_to_all(block, "tmpl", 0, 0).reshape(-1, samples)
-    own = jnp.dot(synthesis[0], piece, preferred_element_type=jnp.float32)
-    other = lax.ppermute(own, "sect", [(0, 1), (1, 0)])
-    return residual_of(own, other, spectrum, weight, forward, inverse, half, share)
+    part = share_products(own_rows, other_rows, mine)
+    return residual_of(
+        own_rows, other_rows, theirs, part, spectrum, weight, forward, inverse, half, samples // sections
+    )
 
 
 def solution(mesh):

time: 40.3 us -> 42.3 us (1.050)
  blocking collectives: 29.5 us -> 0 us
  starting transfers between devices: 2.2 us -> 15.5 us
  waiting for transfers between devices: 1.55 us -> 14.4 us
  Pallas kernels: 3.97 us -> 7.31 us
  local copies, waits for them, and re-layouts: 1.55 us -> 3.93 us
  matrix products: 0.7 us -> 0 us
    all_to_all x1 -> x0, blocking collectives: 29.5 us -> none  [local(): piece = lax.all_to_all(block, 'tmpl', 0, 0).reshape(-1, samples)]
    all_to_all x0 -> x1, waiting for transfers between devices: none -> 14.4 us  [local(): mine = lax.all_to_all(block, 'tmpl', 0, 0).reshape(-1, share)]
    all_to_all x0 -> x1, starting transfers between devices: none -> 11.2 us  [local(): mine = lax.all_to_all(block, 'tmpl', 0, 0).reshape(-1, share)]
    unnamed x12, local copies, waits for them, and re-layouts: 1.55 us -> 3.93 us
    ppermute x1 -> x4, starting transfers between devices: 2.2 us -> 4.25 us  [the longest x1 1.92 us: local(): theirs = lax.ppermute(mine, 'sect', swap)]
    pallas_call x1 -> x3, Pallas kernels: 0.87 us -> 2.82 us  [the longest x1 1.5 us: basis_share(): pl.pallas_call(last_kernel, out_shape=jax.ShapeDtypeStruct((chips, own.sh...]
    ppermute x1 -> x4, waiting for transfers between devices: 1.55 us -> 0.01 us  [the longest x1 0.01 us: local(): other_line = lax.ppermute(strain, 'sect', swap)]
    pallas_call x1, Pallas kernels: 2.37 us -> 3.76 us  [residual_of(): pl.pallas_call(functools.partial(residual_kernel, half), out_shape=(jax.S...]
  transfers between devices with their start and end apart: 1 -> 5, of which waited for: 1 -> 1; matrix products, arithmetic and copies ran while one was open for 0% -> 0% of each run, Pallas kernels for 2% -> 5%
where the time goes in v2:
time: 42.3 us; the launch traced here: 41.8 us
  starting transfers between devices  15.5 us (37%)
  waiting for transfers between devices  14.4 us (34%)
  Pallas kernels  7.31 us (17%)
  local copies, waits for them, and re-layouts  3.93 us (9%)
  between operations  0.72 us (2%)
    all_to_all x1, waiting for transfers between devices, local(): mine = lax.all_to_all(block, 'tmpl', 0, 0).reshape(-1, share)  14.4 us
    all_to_all x1, starting transfers between devices, local(): mine = lax.all_to_all(block, 'tmpl', 0, 0).reshape(-1, share)  11.2 us
    unnamed x12, local copies, waits for them, and re-layouts  3.93 us
    pallas_call x1, Pallas kernels, residual_of(): pl.pallas_call(functools.partial(residual_kernel, half), out_shape=(jax.S...  3.76 us
    ppermute x1, starting transfers between devices, local(): theirs = lax.ppermute(mine, 'sect', swap)  1.92 us
    pallas_call x1, Pallas kernels, basis_share(): pl.pallas_call(last_kernel, out_shape=jax.ShapeDtypeStruct((chips, own.sh...  1.5 us
    ppermute x1, starting transfers between devices, local(): other_line = lax.ppermute(strain, 'sect', swap)  1.46 us
    pallas_call x1, Pallas kernels, share_products(): pl.pallas_call(lambda own_ref, other_ref, basis_ref, out_ref: products(ow...  0.87 us
  transfers between devices with their start and end apart: 5, of which 1 were waited for; matrix products, arithmetic and copies ran while one was open for 0% of the time, Pallas kernels for 5%

profile of v2, /device:TPU:1, one launch (start us, length us, event | category | flops | bytes accessed | tf_op | source)
XLA Modules:
  0.0 41.8 jit_solution(5152969739453429524)
XLA Ops:
  0.6 1.5 %collective-permute-start.1 = (bf16[1,1535]{1,0:T(2,128)(2,1)}, bf16[1,1535]{1,0:T(2,128)(2,1)S(1)}, u32[]{:S(2)}, u32[]{:S(2)}) collective-permute-start(bf16[1,1535]{1,0:T(2,128)(2,1)} %own_line_ref.1), channel_id=1, source_target_pairs={{0,64},{64,0},{1,65},{65,1},{2,66},{66,2},{3,67},{67,3},{4,68},{68... | collective-permute-start | bytes 9218 | tf_op jit(solution)/shard_map/ppermute | solution.py:308
  2.1 0.1 collective-permute-start.2
  2.2 0.0 copy-start.3
  2.2 0.8 %copy-done.3 = bf16[1,16,1024]{2,1,0:T(8,128)(2,1)S(1)} copy-done((bf16[1,16,1024]{2,1,0:T(8,128)(2,1)S(1)}, bf16[1,16,1024]{2,1,0:T(8,128)(2,1)}, u32[]{:S(2)}) %copy-start.3) | copy-done | bytes 32792
  2.9 0.0 copy-start.4
  2.9 0.7 %copy-done.4 = bf16[1,1535]{1,0:T(2,128)(2,1)S(1)} copy-done((bf16[1,1535]{1,0:T(2,128)(2,1)S(1)}, bf16[1,1535]{1,0:T(2,128)(2,1)}, u32[]{:S(2)}) %copy-start.4) | copy-done | bytes 3094
  3.6 0.5 %first_columns.1.first_ref = bf16[16,256]{1,0:T(8,128)(2,1)S(1)} custom-call(bf16[1,1535]{1,0:T(2,128)(2,1)S(1)} %copy-done.4, bf16[16,1024]{1,0:T(8,128)(2,1)S(1)} %bitcast.16), custom_call_target="tpu_custom_call" | custom-call | flops 1073741824 | bytes 4194304 | tf_op jit(solution)/shard_map/first_columns/pallas_call | solution.py:66
  4.1 0.0 copy-start
  4.1 0.0 collective-permute-done.1.other_line_ref
  4.1 0.0 collective-permute-done.2.other_ref
  4.1 1.5 %basis_share.1 = bf16[64,16,384]{2,1,0:T(8,128)(2,1)} custom-call(bf16[1,1535]{1,0:T(2,128)(2,1)S(1)} %copy-done.4, bf16[1,1535]{1,0:T(2,128)(2,1)S(1)} %collective-permute-done.1.other_line_ref, bf16[16,1024]{1,0:T(8,128)(2,1)S(1)} %bitcast.17, bf16[16,1024]{1,0:T(8,128)(2,1)S(1)} %collective-permute-done.2.other_ref, ...), custom_call_target="tpu_custom_call" | custom-call | tf_op jit(solution)/shard_map/basis_share/pallas_call | solution.py:102
  5.6 11.2 %all-to-all-start = ((bf16[64,16,384]{2,1,0:T(8,128)(2,1)}), bf16[64,16,384]{2,1,0:T(8,128)(2,1)S(1)}, u32[]{:S(2)}, u32[]{:S(2)}) async-start(bf16[64,16,384]{2,1,0:T(8,128)(2,1)} %basis_share.1), calls=%async_computation | async-start | bytes 1572864 | tf_op jit(solution)/shard_map/all_to_all | solution.py:313
  16.9 0.0 copy-done
  16.9 0.8 %collective-permute-start = (bf16[512,1024]{1,0:T(8,128)(2,1)S(1)}, bf16[512,1024]{1,0:T(8,128)(2,1)S(1)}, u32[]{:S(2)}, u32[]{:S(2)}) collective-permute-start(bf16[512,1024]{1,0:T(8,128)(2,1)S(1)} %bitcast.10), channel_id=1, source_target_pairs={{0,64},{64,0},{1,65},{65,1},{2,66},{66,2},{3,67},{67,3},{4,68},{68... | collective-permute-start | bytes 3145736 | tf_op jit(solution)/shard_map/ppermute | solution.py:310
  17.7 14.4 %all-to-all-done = bf16[64,16,384]{2,1,0:T(8,128)(2,1)S(1)} async-done(((bf16[64,16,384]{2,1,0:T(8,128)(2,1)}), bf16[64,16,384]{2,1,0:T(8,128)(2,1)S(1)}, u32[]{:S(2)}, u32[]{:S(2)}) %all-to-all-start) | async-done | bytes 786464 | tf_op jit(solution)/shard_map/all_to_all | solution.py:313
  32.1 1.9 %collective-permute-start.3 = (bf16[1024,384]{1,0:T(8,128)(2,1)S(1)}, bf16[1024,384]{1,0:T(8,128)(2,1)S(1)}, u32[]{:S(2)}, u32[]{:S(2)}) collective-permute-start(bf16[1024,384]{1,0:T(8,128)(2,1)S(1)} %bitcast.13), channel_id=1, source_target_pairs={{0,64},{64,0},{1,65},{65,1},{2,66},{66,2},{3,67},{67,3},{4,68},{68... | collective-permute-start | bytes 2359304 | tf_op jit(solution)/shard_map/ppermute | solution.py:314
  34.0 0.0 copy-start.1
  34.0 1.1 %copy-done.1 = bf16[512,768]{1,0:T(8,128)(2,1)S(1)} copy-done((bf16[512,768]{1,0:T(8,128)(2,1)S(1)}, bf16[512,768]{1,0:T(8,128)(2,1)}, u32[]{:S(2)}) %copy-start.1) | copy-done | bytes 786456
  35.1 0.0 copy-start.5
  35.1 1.1 %copy-done.5 = f32[256,2,351]{0,1,2:T(2,128)S(1)} copy-done((f32[256,2,351]{0,1,2:T(2,128)S(1)}, f32[256,2,351]{0,1,2:T(2,128)}, u32[]{:S(2)}) %copy-start.5) | copy-done | bytes 718872
  36.2 0.7 %lag_spectrum.1 = (f32[512,768]{1,0:T(8,128)S(1)}, f32[256,128]{1,0:T(8,128)S(1)}) custom-call(f32[351,4,128]{2,1,0:T(4,128)S(1)} %bitcast.18, bf16[512,768]{1,0:T(8,128)(2,1)S(1)} %copy-done.1), custom_call_target="tpu_custom_call" | custom-call | flops 1073741824 | bytes 4194304 | tf_op jit(solution)/shard_map/lag_spectrum/pallas_call | solution.py:157
  36.9 0.0 copy-start.2
  37.0 0.0 collective-permute-done.other_ref
  37.0 0.9 %share_products.1.part_ref = f32[512,384]{1,0:T(8,128)S(1)} custom-call(bf16[512,1024]{1,0:T(8,128)(2,1)S(1)} %bitcast.11, bf16[512,1024]{1,0:T(8,128)(2,1)S(1)} %collective-permute-done.other_ref, bf16[1024,384]{1,0:T(8,128)(2,1)S(1)} %bitcast.14), custom_call_target="tpu_custom_call" | custom-call | flops 1073741824 | bytes 4194304 | tf_op jit(solution)/shard_map/share_products/pallas_call | solution.py:172
  37.8 0.0 collective-permute-done.3.basis_ref
  37.8 0.2 copy-done.2
  38.1 3.8 %residual.1 = (bf16[512,256]{1,0:T(8,128)(2,1)}, f32[256,256]{1,0:T(8,128)}) custom-call(bf16[512,1024]{1,0:T(8,128)(2,1)S(1)} %bitcast.12, bf16[512,1024]{1,0:T(8,128)(2,1)S(1)} %collective-permute-done.other_ref, bf16[1024,384]{1,0:T(8,128)(2,1)S(1)} %collective-permute-done.3.basis_ref, f32[512,384]{1,0:T(8,128)S(1)} %share_products.1.part_ref, ...), custom_call_target="tpu_custom_call" | custom-call | tf_op jit(solution)/shard_map/residual/pallas_call | solution.py:280
Async XLA Ops:
  0.6 3.5 %collective-permute-start.1 = (bf16[1,1535]{1,0:T(2,128)(2,1)}, bf16[1,1535]{1,0:T(2,128)(2,1)S(1)}, u32[]{:S(2)}, u32[]{:S(2)}) collective-permute-start(bf16[1,1535]{1,0:T(2,128)(2,1)} %own_line_ref.1), channel_id=1, source_target_pairs={{0,64},{64,0},{1,65},{65,1},{2,66},{66,2},{3,67},{67,3},{4,68},{68... | collective-permute-start | bytes 9218 | tf_op jit(solution)/shard_map/ppermute | solution.py:308
  2.1 2.0 %collective-permute-start.2 = (bf16[16,1024]{1,0:T(8,128)(2,1)}, bf16[16,1024]{1,0:T(8,128)(2,1)S(1)}, u32[]{:S(2)}, u32[]{:S(2)}) collective-permute-start(bf16[16,1024]{1,0:T(8,128)(2,1)} %bitcast.15), channel_id=1, source_target_pairs={{0,64},{64,0},{1,65},{65,1},{2,66},{66,2},{3,67},{67,3},{4,68},{68... | collective-permute-start | bytes 98312 | tf_op jit(solution)/shard_map/ppermute | solution.py:309
  2.2 0.8 %copy-start.3 = (bf16[1,16,1024]{2,1,0:T(8,128)(2,1)S(1)}, bf16[1,16,1024]{2,1,0:T(8,128)(2,1)}, u32[]{:S(2)}) copy-start(bf16[1,16,1024]{2,1,0:T(8,128)(2,1)} %param.7) | copy-start | bytes 98308
  2.9 0.7 %copy-start.4 = (bf16[1,1535]{1,0:T(2,128)(2,1)S(1)}, bf16[1,1535]{1,0:T(2,128)(2,1)}, u32[]{:S(2)}) copy-start(bf16[1,1535]{1,0:T(2,128)(2,1)} %own_line_ref.1) | copy-start | bytes 9214
  4.1 12.8 %copy-start = (bf16[1,512,1024]{2,1,0:T(8,128)(2,1)S(1)}, bf16[1,512,1024]{2,1,0:T(8,128)(2,1)}, u32[]{:S(2)}) copy-start(bf16[1,512,1024]{2,1,0:T(8,128)(2,1)} %param.8) | copy-start | bytes 3145732
  5.6 26.4 %all-to-all-start = ((bf16[64,16,384]{2,1,0:T(8,128)(2,1)}), bf16[64,16,384]{2,1,0:T(8,128)(2,1)S(1)}, u32[]{:S(2)}, u32[]{:S(2)}) async-start(bf16[64,16,384]{2,1,0:T(8,128)(2,1)} %basis_share.1), calls=%async_computation | async-start | bytes 1572864 | tf_op jit(solution)/shard_map/all_to_all | solution.py:313
  16.9 20.1 %collective-permute-start = (bf16[512,1024]{1,0:T(8,128)(2,1)S(1)}, bf16[512,1024]{1,0:T(8,128)(2,1)S(1)}, u32[]{:S(2)}, u32[]{:S(2)}) collective-permute-start(bf16[512,1024]{1,0:T(8,128)(2,1)S(1)} %bitcast.10), channel_id=1, source_target_pairs={{0,64},{64,0},{1,65},{65,1},{2,66},{66,2},{3,67},{67,3},{4,68},{68... | collective-permute-start | bytes 3145736 | tf_op jit(solution)/shard_map/ppermute | solution.py:310
  32.1 5.8 %collective-permute-start.3 = (bf16[1024,384]{1,0:T(8,128)(2,1)S(1)}, bf16[1024,384]{1,0:T(8,128)(2,1)S(1)}, u32[]{:S(2)}, u32[]{:S(2)}) collective-permute-start(bf16[1024,384]{1,0:T(8,128)(2,1)S(1)} %bitcast.13), channel_id=1, source_target_pairs={{0,64},{64,0},{1,65},{65,1},{2,66},{66,2},{3,67},{67,3},{4,68},{68... | collective-permute-start | bytes 2359304 | tf_op jit(solution)/shard_map/ppermute | solution.py:314
  34.0 1.1 %copy-start.1 = (bf16[512,768]{1,0:T(8,128)(2,1)S(1)}, bf16[512,768]{1,0:T(8,128)(2,1)}, u32[]{:S(2)}) copy-start(bf16[512,768]{1,0:T(8,128)(2,1)} %constant.4.clone.forward_ref) | copy-start | bytes 2359300
  35.1 1.1 %copy-start.5 = (f32[256,2,351]{0,1,2:T(2,128)S(1)}, f32[256,2,351]{0,1,2:T(2,128)}, u32[]{:S(2)}) copy-start(f32[256,2,351]{0,1,2:T(2,128)} %param.9) | copy-start | bytes 2156548
  36.9 1.1 %copy-start.2 = (bf16[768,512]{1,0:T(8,128)(2,1)S(1)}, bf16[768,512]{1,0:T(8,128)(2,1)}, u32[]{:S(2)}) copy-start(bf16[768,512]{1,0:T(8,128)(2,1)} %constant.5.clone.inverse_ref) | copy-start | bytes 2359300

commit v3 on v2

--- a/solution.py
+++ b/solution.py
@@ -76,7 +76,7 @@
         compiler_params=pltpu.CompilerParams(vmem_limit_bytes=GRANT),
         cost_estimate=pl.CostEstimate(flops=1 << 30, bytes_accessed=1 << 22, transcendentals=0),
         name="first_columns",
-    )(line, bank)
+    )(pltpu.with_memory_space_constraint(line, pltpu.HBM), pltpu.with_memory_space_constraint(bank, pltpu.HBM))
 
 
 def last_kernel(own_line_ref, other_line_ref, own_ref, other_ref, first_ref, basis_ref, line_ref):
@@ -145,8 +145,13 @@
     ones = jnp.ones((length, lanes), jnp.bfloat16)
     weight_ref[...] = rows_dot(high, ones) + rows_dot(low, ones)
     table = forward_ref[0:length, :]
-    spectrum_ref[0:groups, :] = rows_dot(real_part.astype(jnp.bfloat16), table)
-    spectrum_ref[groups:, :] = rows_dot(imag_part.astype(jnp.bfloat16), table)
+    scale = jnp.float32(1.0 / PERIOD)
+    real_hat = rows_dot(real_part.astype(jnp.bfloat16), table) * scale
+    imag_hat = rows_dot(imag_part.astype(jnp.bfloat16), table) * scale
+    spectrum_ref[0:groups, 0:BINS] = real_hat[:, :BINS] - imag_hat[:, BINS:]
+    spectrum_ref[0:groups, BINS:] = real_hat[:, BINS:] + imag_hat[:, :BINS]
+    spectrum_ref[groups:, 0:BINS] = real_hat[:, :BINS] + imag_hat[:, BINS:]
+    spectrum_ref[groups:, BINS:] = real_hat[:, BINS:] - imag_hat[:, :BINS]
 
 
 def lag_spectrum(correlation, forward):
@@ -192,7 +197,6 @@
     residual_ref,
     full_ref,
     rest_ref,
-    slow_ref,
 ):
     section = lax.axis_index("sect")
     groups, share = residual_ref.shape
@@ -202,12 +206,19 @@
     wide = basis_ref.shape[1] - LANES
     products(other_ref, own_ref, other_ref, basis_ref, rest_ref)
 
+    lane = lax.broadcasted_iota(jnp.int32, (2 * groups, LANES), 1)
+
     def placed(slow, middle, left, right):
-        slow_ref[...] = slow[:, 0:wide]
-        full_ref[0] = left[:, wide:]
-        for tile in range(1, tiles - 1):
-            full_ref[tile] = middle[:, (tile - 1) * LANES : tile * LANES]
-        full_ref[tiles - 1] = right[:, wide:]
+        for tile in range(tiles):
+            start = (tile // 2) * LANES
+            held = jnp.take_along_axis(slow[:, start : start + LANES], lane // 2 + (tile % 2) * (LANES // 2), axis=1)
+            if tile == 0:
+                fast = left[:, wide:]
+            elif tile == tiles - 1:
+                fast = right[:, wide:]
+            else:
+                fast = middle[:, (tile - 1) * LANES : tile * LANES]
+            full_ref[tile] = held + fast
 
     @pl.when(section == 0)
     def _():
@@ -217,14 +228,6 @@
     def _():
         placed(rest_ref, part_ref, rest_ref, part_ref)
 
-    source = lax.broadcasted_iota(jnp.int32, (wide, samples), 0)
-    target = lax.broadcasted_iota(jnp.int32, (wide, samples), 1)
-    hold = (source == target // 2).astype(jnp.float32).astype(jnp.bfloat16)
-    high, low = split(slow_ref[...])
-    held = jnp.dot(high, hold, preferred_element_type=jnp.float32)
-    held += jnp.dot(low, hold, preferred_element_type=jnp.float32)
-    for tile in range(tiles):
-        full_ref[tile] += held[:, tile * LANES : (tile + 1) * LANES]
     first = pl.multiple_of(section * share, share)
     mine = pl.ds(first, share)
     own_tiles = [section * (share // LANES) + step for step in range(share // LANES)]
@@ -253,21 +256,20 @@
     b_real, b_imag = imag_hat[:, :BINS], imag_hat[:, BINS:]
     p_real, p_imag = spectrum_ref[0:groups, 0:BINS], spectrum_ref[0:groups, BINS:]
     q_real, q_imag = spectrum_ref[groups:, 0:BINS], spectrum_ref[groups:, BINS:]
-    scale = jnp.float32(2.0 / PERIOD)
     back = inverse_ref[:, mine]
 
     def turned(low_part, high_part):
-        parts = jnp.concatenate([low_part * scale, high_part * scale], axis=1).astype(jnp.bfloat16)
+        parts = jnp.concatenate([low_part, high_part], axis=1).astype(jnp.bfloat16)
         return jnp.dot(parts, back, preferred_element_type=jnp.float32)
 
-    real_sum = turned(
-        a_real * p_real + a_imag * p_imag + b_real * q_real + b_imag * q_imag,
-        a_imag * p_real - a_real * p_imag + b_imag * q_real - b_real * q_imag,
-    )
-    imag_sum = turned(
-        b_real * p_real + b_imag * p_imag - a_real * q_real - a_imag * q_imag,
-        b_imag * p_real - b_real * p_imag - a_imag * q_real + a_real * q_imag,
-    )
+    up_real, up_imag = a_real - b_imag, a_imag + b_real
+    down_real, down_imag = a_real + b_imag, a_imag - b_real
+    plus_real = up_real * p_real + up_imag * p_imag
+    plus_imag = up_imag * p_real - up_real * p_imag
+    minus_real = down_real * q_real + down_imag * q_imag
+    minus_imag = down_imag * q_real - down_real * q_imag
+    real_sum = turned(plus_real + minus_real, plus_imag + minus_imag)
+    imag_sum = turned(plus_imag - minus_imag, minus_real - plus_real)
     cross = real_mid * real_sum + imag_mid * imag_sum
     magnitude = real_mid * real_mid + imag_mid * imag_mid
     weight = jnp.concatenate([weight_ref[...]] * (share // LANES), axis=1)
@@ -276,7 +278,6 @@
 
 def residual_of(own, other, basis, part, spectrum, weight, forward, inverse, half, share):
     columns = own.shape[0]
-    wide = basis.shape[1] - LANES
     return pl.pallas_call(
         functools.partial(residual_kernel, half),
         out_shape=(
@@ -286,7 +287,6 @@
         scratch_shapes=[
             pltpu.VMEM((forward.shape[0] // LANES, columns, LANES), jnp.float32),
             pltpu.VMEM(part.shape, jnp.float32),
-            pltpu.VMEM((columns, wide), jnp.float32),
         ],
         compiler_params=pltpu.CompilerParams(vmem_limit_bytes=GRANT),
         name="residual",

time: 42.3 us -> 41.1 us (0.972)
  local copies, waits for them, and re-layouts: 3.93 us -> 2.49 us
    unnamed x12, local copies, waits for them, and re-layouts: 3.93 us -> 2.49 us
    pallas_call x1, Pallas kernels: 0.46 us -> 1.19 us  [first_columns(): pl.pallas_call(first_kernel, in_specs=[pl.BlockSpec(memory_space=pltpu.HB...]
    pallas_call x1, Pallas kernels: 3.76 us -> 3.25 us  [residual_of(): pl.pallas_call(functools.partial(residual_kernel, half), out_shape=(jax.S...]
  transfers between devices with their start and end apart: 5 -> 5, of which waited for: 1 -> 2; matrix products, arithmetic and copies ran while one was open for 0% -> 0% of each run, Pallas kernels for 5% -> 7%
where the time goes in v3:
time: 41.1 us; the launch traced here: 40.7 us
  starting transfers between devices  15.4 us (37%)
  waiting for transfers between devices  14.6 us (36%)
  Pallas kernels  7.56 us (18%)
  local copies, waits for them, and re-layouts  2.49 us (6%)
  between operations  0.72 us (2%)
    all_to_all x1, waiting for transfers between devices, local(): mine = lax.all_to_all(block, 'tmpl', 0, 0).reshape(-1, share)  14.5 us
    all_to_all x1, starting transfers between devices, local(): mine = lax.all_to_all(block, 'tmpl', 0, 0).reshape(-1, share)  11.2 us
    pallas_call x1, Pallas kernels, residual_of(): pl.pallas_call(functools.partial(residual_kernel, half), out_shape=(jax.S...  3.25 us
    unnamed x12, local copies, waits for them, and re-layouts  2.49 us
    ppermute x1, starting transfers between devices, local(): theirs = lax.ppermute(mine, 'sect', swap)  1.85 us
    pallas_call x1, Pallas kernels, basis_share(): pl.pallas_call(last_kernel, out_shape=jax.ShapeDtypeStruct((chips, own.sh...  1.5 us
    ppermute x1, starting transfers between devices, local(): other_line = lax.ppermute(strain, 'sect', swap)  1.46 us
    pallas_call x1, Pallas kernels, first_columns(): pl.pallas_call(first_kernel, in_specs=[pl.BlockSpec(memory_space=pltpu.HB...  1.19 us
  transfers between devices with their start and end apart: 5, of which 2 were waited for; matrix products, arithmetic and copies ran while one was open for 0% of the time, Pallas kernels for 7%

profile of v3, /device:TPU:1, one launch (start us, length us, event | category | flops | bytes accessed | tf_op | source)
XLA Modules:
  0.0 40.7 jit_solution(9057009483225304642)
XLA Ops:
  0.6 1.5 %collective-permute-start.1 = (bf16[1,1535]{1,0:T(2,128)(2,1)}, bf16[1,1535]{1,0:T(2,128)(2,1)S(1)}, u32[]{:S(2)}, u32[]{:S(2)}) collective-permute-start(bf16[1,1535]{1,0:T(2,128)(2,1)} %own_line_ref.1), channel_id=1, source_target_pairs={{0,64},{64,0},{1,65},{65,1},{2,66},{66,2},{3,67},{67,3},{4,68},{68... | collective-permute-start | bytes 9218 | tf_op jit(solution)/shard_map/ppermute | solution.py:308
  2.1 0.0 copy-start.3
  2.1 0.0 copy-start.4
  2.1 0.1 collective-permute-start.2
  2.2 1.2 %first_columns.1.first_ref = bf16[16,256]{1,0:T(8,128)(2,1)S(1)} custom-call(bf16[1,1535]{1,0:T(2,128)(2,1)} %own_line_ref.1, bf16[16,1024]{1,0:T(8,128)(2,1)} %bitcast.16), custom_call_target="tpu_custom_call" | custom-call | flops 1073741824 | bytes 4194304 | tf_op jit(solution)/shard_map/first_columns/pallas_call | solution.py:66
  3.4 0.0 copy-start
  3.4 0.0 collective-permute-done.1.other_line_ref
  3.4 0.1 collective-permute-done.2.other_ref
  3.5 0.0 copy-done.3
  3.5 0.0 copy-done.4
  3.5 1.5 %basis_share.1 = bf16[64,16,384]{2,1,0:T(8,128)(2,1)} custom-call(bf16[1,1535]{1,0:T(2,128)(2,1)S(1)} %copy-done.4, bf16[1,1535]{1,0:T(2,128)(2,1)S(1)} %collective-permute-done.1.other_line_ref, bf16[16,1024]{1,0:T(8,128)(2,1)S(1)} %bitcast.17, bf16[16,1024]{1,0:T(8,128)(2,1)S(1)} %collective-permute-done.2.other_ref, ...), custom_call_target="tpu_custom_call" | custom-call | tf_op jit(solution)/shard_map/basis_share/pallas_call | solution.py:102
  5.0 11.2 %all-to-all-start = ((bf16[64,16,384]{2,1,0:T(8,128)(2,1)}), bf16[64,16,384]{2,1,0:T(8,128)(2,1)S(1)}, u32[]{:S(2)}, u32[]{:S(2)}) async-start(bf16[64,16,384]{2,1,0:T(8,128)(2,1)} %basis_share.1), calls=%async_computation | async-start | bytes 1572864 | tf_op jit(solution)/shard_map/all_to_all | solution.py:313
  16.3 0.0 copy-done
  16.3 0.7 %collective-permute-start = (bf16[512,1024]{1,0:T(8,128)(2,1)S(1)}, bf16[512,1024]{1,0:T(8,128)(2,1)S(1)}, u32[]{:S(2)}, u32[]{:S(2)}) collective-permute-start(bf16[512,1024]{1,0:T(8,128)(2,1)S(1)} %bitcast.10), channel_id=1, source_target_pairs={{0,64},{64,0},{1,65},{65,1},{2,66},{66,2},{3,67},{67,3},{4,68},{68... | collective-permute-start | bytes 3145736 | tf_op jit(solution)/shard_map/ppermute | solution.py:310
  17.0 14.5 %all-to-all-done = bf16[64,16,384]{2,1,0:T(8,128)(2,1)S(1)} async-done(((bf16[64,16,384]{2,1,0:T(8,128)(2,1)}), bf16[64,16,384]{2,1,0:T(8,128)(2,1)S(1)}, u32[]{:S(2)}, u32[]{:S(2)}) %all-to-all-start) | async-done | bytes 786464 | tf_op jit(solution)/shard_map/all_to_all | solution.py:313
  31.5 1.8 %collective-permute-start.3 = (bf16[1024,384]{1,0:T(8,128)(2,1)S(1)}, bf16[1024,384]{1,0:T(8,128)(2,1)S(1)}, u32[]{:S(2)}, u32[]{:S(2)}) collective-permute-start(bf16[1024,384]{1,0:T(8,128)(2,1)S(1)} %bitcast.13), channel_id=1, source_target_pairs={{0,64},{64,0},{1,65},{65,1},{2,66},{66,2},{3,67},{67,3},{4,68},{68... | collective-permute-start | bytes 2359304 | tf_op jit(solution)/shard_map/ppermute | solution.py:314
  33.4 0.0 copy-start.1
  33.4 1.1 %copy-done.1 = bf16[512,768]{1,0:T(8,128)(2,1)S(1)} copy-done((bf16[512,768]{1,0:T(8,128)(2,1)S(1)}, bf16[512,768]{1,0:T(8,128)(2,1)}, u32[]{:S(2)}) %copy-start.1) | copy-done | bytes 786456
  34.5 0.0 copy-start.5
  34.5 1.1 %copy-done.5 = f32[256,2,351]{0,1,2:T(2,128)S(1)} copy-done((f32[256,2,351]{0,1,2:T(2,128)S(1)}, f32[256,2,351]{0,1,2:T(2,128)}, u32[]{:S(2)}) %copy-start.5) | copy-done | bytes 718872
  35.6 0.7 %lag_spectrum.1 = (f32[512,768]{1,0:T(8,128)S(1)}, f32[256,128]{1,0:T(8,128)S(1)}) custom-call(f32[351,4,128]{2,1,0:T(4,128)S(1)} %bitcast.18, bf16[512,768]{1,0:T(8,128)(2,1)S(1)} %copy-done.1), custom_call_target="tpu_custom_call" | custom-call | flops 1073741824 | bytes 4194304 | tf_op jit(solution)/shard_map/lag_spectrum/pallas_call | solution.py:162
  36.4 0.0 copy-start.2
  36.4 0.0 collective-permute-done.other_ref
  36.4 0.9 %share_products.1.part_ref = f32[512,384]{1,0:T(8,128)S(1)} custom-call(bf16[512,1024]{1,0:T(8,128)(2,1)S(1)} %bitcast.11, bf16[512,1024]{1,0:T(8,128)(2,1)S(1)} %collective-permute-done.other_ref, bf16[1024,384]{1,0:T(8,128)(2,1)S(1)} %bitcast.14), custom_call_target="tpu_custom_call" | custom-call | flops 1073741824 | bytes 4194304 | tf_op jit(solution)/shard_map/share_products/pallas_call | solution.py:177
  37.2 0.0 collective-permute-done.3.basis_ref
  37.3 0.2 copy-done.2
  37.5 3.2 %residual.1 = (bf16[512,256]{1,0:T(8,128)(2,1)}, f32[256,256]{1,0:T(8,128)}) custom-call(bf16[512,1024]{1,0:T(8,128)(2,1)S(1)} %bitcast.12, bf16[512,1024]{1,0:T(8,128)(2,1)S(1)} %collective-permute-done.other_ref, bf16[1024,384]{1,0:T(8,128)(2,1)S(1)} %collective-permute-done.3.basis_ref, f32[512,384]{1,0:T(8,128)S(1)} %share_products.1.part_ref, ...), custom_call_target="tpu_custom_call" | custom-call | tf_op jit(solution)/shard_map/residual/pallas_call | solution.py:281
Async XLA Ops:
  0.6 2.8 %collective-permute-start.1 = (bf16[1,1535]{1,0:T(2,128)(2,1)}, bf16[1,1535]{1,0:T(2,128)(2,1)S(1)}, u32[]{:S(2)}, u32[]{:S(2)}) collective-permute-start(bf16[1,1535]{1,0:T(2,128)(2,1)} %own_line_ref.1), channel_id=1, source_target_pairs={{0,64},{64,0},{1,65},{65,1},{2,66},{66,2},{3,67},{67,3},{4,68},{68... | collective-permute-start | bytes 9218 | tf_op jit(solution)/shard_map/ppermute | solution.py:308
  2.1 1.4 %copy-start.3 = (bf16[1,16,1024]{2,1,0:T(8,128)(2,1)S(1)}, bf16[1,16,1024]{2,1,0:T(8,128)(2,1)}, u32[]{:S(2)}) copy-start(bf16[1,16,1024]{2,1,0:T(8,128)(2,1)} %param.7) | copy-start | bytes 98308
  2.1 1.4 %copy-start.4 = (bf16[1,1535]{1,0:T(2,128)(2,1)S(1)}, bf16[1,1535]{1,0:T(2,128)(2,1)}, u32[]{:S(2)}) copy-start(bf16[1,1535]{1,0:T(2,128)(2,1)} %own_line_ref.1) | copy-start | bytes 9214
  2.1 1.4 %collective-permute-start.2 = (bf16[16,1024]{1,0:T(8,128)(2,1)}, bf16[16,1024]{1,0:T(8,128)(2,1)S(1)}, u32[]{:S(2)}, u32[]{:S(2)}) collective-permute-start(bf16[16,1024]{1,0:T(8,128)(2,1)} %bitcast.15), channel_id=1, source_target_pairs={{0,64},{64,0},{1,65},{65,1},{2,66},{66,2},{3,67},{67,3},{4,68},{68... | collective-permute-start | bytes 98312 | tf_op jit(solution)/shard_map/ppermute | solution.py:309
  3.4 12.9 %copy-start = (bf16[1,512,1024]{2,1,0:T(8,128)(2,1)S(1)}, bf16[1,512,1024]{2,1,0:T(8,128)(2,1)}, u32[]{:S(2)}) copy-start(bf16[1,512,1024]{2,1,0:T(8,128)(2,1)} %param.8) | copy-start | bytes 3145732
  5.0 26.5 %all-to-all-start = ((bf16[64,16,384]{2,1,0:T(8,128)(2,1)}), bf16[64,16,384]{2,1,0:T(8,128)(2,1)S(1)}, u32[]{:S(2)}, u32[]{:S(2)}) async-start(bf16[64,16,384]{2,1,0:T(8,128)(2,1)} %basis_share.1), calls=%async_computation | async-start | bytes 1572864 | tf_op jit(solution)/shard_map/all_to_all | solution.py:313
  16.3 20.1 %collective-permute-start = (bf16[512,1024]{1,0:T(8,128)(2,1)S(1)}, bf16[512,1024]{1,0:T(8,128)(2,1)S(1)}, u32[]{:S(2)}, u32[]{:S(2)}) collective-permute-start(bf16[512,1024]{1,0:T(8,128)(2,1)S(1)} %bitcast.10), channel_id=1, source_target_pairs={{0,64},{64,0},{1,65},{65,1},{2,66},{66,2},{3,67},{67,3},{4,68},{68... | collective-permute-start | bytes 3145736 | tf_op jit(solution)/shard_map/ppermute | solution.py:310
  31.5 5.7 %collective-permute-start.3 = (bf16[1024,384]{1,0:T(8,128)(2,1)S(1)}, bf16[1024,384]{1,0:T(8,128)(2,1)S(1)}, u32[]{:S(2)}, u32[]{:S(2)}) collective-permute-start(bf16[1024,384]{1,0:T(8,128)(2,1)S(1)} %bitcast.13), channel_id=1, source_target_pairs={{0,64},{64,0},{1,65},{65,1},{2,66},{66,2},{3,67},{67,3},{4,68},{68... | collective-permute-start | bytes 2359304 | tf_op jit(solution)/shard_map/ppermute | solution.py:314
  33.4 1.1 %copy-start.1 = (bf16[512,768]{1,0:T(8,128)(2,1)S(1)}, bf16[512,768]{1,0:T(8,128)(2,1)}, u32[]{:S(2)}) copy-start(bf16[512,768]{1,0:T(8,128)(2,1)} %constant.4.clone.forward_ref) | copy-start | bytes 2359300
  34.5 1.1 %copy-start.5 = (f32[256,2,351]{0,1,2:T(2,128)S(1)}, f32[256,2,351]{0,1,2:T(2,128)}, u32[]{:S(2)}) copy-start(f32[256,2,351]{0,1,2:T(2,128)} %param.9) | copy-start | bytes 2156548
  36.4 1.1 %copy-start.2 = (bf16[768,512]{1,0:T(8,128)(2,1)S(1)}, bf16[768,512]{1,0:T(8,128)(2,1)}, u32[]{:S(2)}) copy-start(bf16[768,512]{1,0:T(8,128)(2,1)} %constant.5.clone.inverse_ref) | copy-start | bytes 2359300

commit v4 on v3

--- a/solution.py
+++ b/solution.py
@@ -13,6 +13,7 @@
 BINS = 384
 LANES = 128
 GRANT = 24 << 20
+SENT = jnp.float32
 
 
 def forward_matrix(rows):
@@ -117,18 +118,42 @@
     return lax.dot_general(left, right, (((0,), (0,)), ((), ())), preferred_element_type=jnp.float32)
 
 
-def products(rows_ref, fast_own_ref, fast_other_ref, basis_ref, out_ref):
+def wide_kernel(own_ref, basis_ref, kept_ref, sent_ref):
+    wide = kept_ref.shape[1]
+    value = jnp.dot(own_ref[...], basis_ref[:, 0:wide], preferred_element_type=jnp.float32)
+    kept_ref[...] = value
+    sent_ref[...] = value.astype(sent_ref.dtype)
+
+
+def narrow_kernel(own_ref, other_ref, basis_ref, kept_ref, sent_ref):
     section = lax.axis_index("sect")
     wide = basis_ref.shape[1] - LANES
-    out_ref[:, 0:wide] = jnp.dot(rows_ref[...], basis_ref[:, 0:wide], preferred_element_type=jnp.float32)
+
+    def multiply(fast_ref):
+        value = jnp.dot(fast_ref[...], basis_ref[:, wide:], preferred_element_type=jnp.float32)
+        kept_ref[...] = value
+        sent_ref[...] = value.astype(sent_ref.dtype)
 
     @pl.when(section == 0)
     def _():
-        out_ref[:, wide:] = jnp.dot(fast_other_ref[...], basis_ref[:, wide:], preferred_element_type=jnp.float32)
+        multiply(other_ref)
 
     @pl.when(section == 1)
     def _():
-        out_ref[:, wide:] = jnp.dot(fast_own_ref[...], basis_ref[:, wide:], preferred_element_type=jnp.float32)
+        multiply(own_ref)
+
+
+def partial_products(kernel, count, *operands):
+    columns = operands[0].shape[0]
+    return pl.pallas_call(
+        kernel,
+        out_shape=(
+            jax.ShapeDtypeStruct((columns, count), jnp.float32),
+            jax.ShapeDtypeStruct((columns, count), SENT),
+        ),
+        compiler_params=pltpu.CompilerParams(vmem_limit_bytes=GRANT),
+        cost_estimate=pl.CostEstimate(flops=1 << 29, bytes_accessed=1 << 21, transcendentals=0),
+    )(*operands)
 
 
 def lags_kernel(series_ref, forward_ref, spectrum_ref, weight_ref):
@@ -171,24 +196,12 @@
     )(series, forward)
 
 
-def share_products(own, other, basis):
-    columns = own.shape[0]
-    share = basis.shape[1]
-    return pl.pallas_call(
-        lambda own_ref, other_ref, basis_ref, out_ref: products(own_ref, own_ref, other_ref, basis_ref, out_ref),
-        out_shape=jax.ShapeDtypeStruct((columns, share), jnp.float32),
-        compiler_params=pltpu.CompilerParams(vmem_limit_bytes=GRANT),
-        cost_estimate=pl.CostEstimate(flops=1 << 30, bytes_accessed=1 << 22, transcendentals=0),
-        name="share_products",
-    )(own, other, basis)
-
-
 def residual_kernel(
     half,
-    own_ref,
-    other_ref,
-    basis_ref,
-    part_ref,
+    own_wide_ref,
+    own_narrow_ref,
+    other_wide_ref,
+    other_narrow_ref,
     spectrum_ref,
     weight_ref,
     forward_ref,
@@ -196,37 +209,34 @@
     snr_ref,
     residual_ref,
     full_ref,
-    rest_ref,
 ):
     section = lax.axis_index("sect")
     groups, share = residual_ref.shape
     samples = forward_ref.shape[0]
     length = 2 * half + 1
     tiles = samples // LANES
-    wide = basis_ref.shape[1] - LANES
-    products(other_ref, own_ref, other_ref, basis_ref, rest_ref)
-
     lane = lax.broadcasted_iota(jnp.int32, (2 * groups, LANES), 1)
 
     def placed(slow, middle, left, right):
         for tile in range(tiles):
             start = (tile // 2) * LANES
-            held = jnp.take_along_axis(slow[:, start : start + LANES], lane // 2 + (tile % 2) * (LANES // 2), axis=1)
+            picked = slow[:, start : start + LANES].astype(jnp.float32)
+            held = jnp.take_along_axis(picked, lane // 2 + (tile % 2) * (LANES // 2), axis=1)
             if tile == 0:
-                fast = left[:, wide:]
+                fast = left[...]
             elif tile == tiles - 1:
-                fast = right[:, wide:]
+                fast = right[...]
             else:
                 fast = middle[:, (tile - 1) * LANES : tile * LANES]
-            full_ref[tile] = held + fast
+            full_ref[tile] = held + fast.astype(jnp.float32)
 
     @pl.when(section == 0)
     def _():
-        placed(part_ref, rest_ref, part_ref, rest_ref)
+        placed(own_wide_ref, other_wide_ref, own_narrow_ref, other_narrow_ref)
 
     @pl.when(section == 1)
     def _():
-        placed(rest_ref, part_ref, rest_ref, part_ref)
+        placed(other_wide_ref, own_wide_ref, other_narrow_ref, own_narrow_ref)
 
     first = pl.multiple_of(section * share, share)
     mine = pl.ds(first, share)
@@ -276,21 +286,18 @@
     residual_ref[...] = (energy - 2.0 * cross + magnitude * weight) * jnp.float32(1.0 / (2.0 * length))
 
 
-def residual_of(own, other, basis, part, spectrum, weight, forward, inverse, half, share):
-    columns = own.shape[0]
+def residual_of(pieces, spectrum, weight, forward, inverse, half, share):
+    columns = pieces[0].shape[0]
     return pl.pallas_call(
         functools.partial(residual_kernel, half),
         out_shape=(
             jax.ShapeDtypeStruct((columns, share), jnp.bfloat16),
             jax.ShapeDtypeStruct((columns // 2, share), jnp.float32),
         ),
-        scratch_shapes=[
-            pltpu.VMEM((forward.shape[0] // LANES, columns, LANES), jnp.float32),
-            pltpu.VMEM(part.shape, jnp.float32),
-        ],
+        scratch_shapes=[pltpu.VMEM((forward.shape[0] // LANES, columns, LANES), jnp.float32)],
         compiler_params=pltpu.CompilerParams(vmem_limit_bytes=GRANT),
         name="residual",
-    )(own, other, basis, part, spectrum, weight, forward, inverse)
+    )(*pieces, spectrum, weight, forward, inverse)
 
 
 def local(strain, filters, synthesis, correlation):
@@ -311,12 +318,13 @@
     first = first_columns(strain, own_bank, share - LANES)
     block = basis_share(strain, other_line, own_bank, other_bank, first, chips)
     mine = lax.all_to_all(block, "tmpl", 0, 0).reshape(-1, share)
-    theirs = lax.ppermute(mine, "sect", swap)
+    own_wide, sent_wide = partial_products(wide_kernel, share - LANES, own_rows, mine)
+    other_wide = lax.ppermute(sent_wide, "sect", swap)
+    own_narrow, sent_narrow = partial_products(narrow_kernel, LANES, own_rows, other_rows, mine)
+    other_narrow = lax.ppermute(sent_narrow, "sect", swap)
     spectrum, weight = lag_spectrum(correlation, forward)
-    part = share_products(own_rows, other_rows, mine)
-    return residual_of(
-        own_rows, other_rows, theirs, part, spectrum, weight, forward, inverse, half, samples // sections
-    )
+    pieces = (own_wide, own_narrow, other_wide, other_narrow)
+    return residual_of(pieces, spectrum, weight, forward, inverse, half, samples // sections)
 
 
 def solution(mesh):

time: 41.1 us -> 37.9 us (0.922)
  blocking collectives: 0 us -> 26.6 us
  waiting for transfers between devices: 14.6 us -> 0.74 us
  starting transfers between devices: 15.4 us -> 3.73 us
  local copies, waits for them, and re-layouts: 2.49 us -> 0.03 us
  Pallas kernels: 7.56 us -> 5.8 us
    all_to_all x0 -> x1, blocking collectives: none -> 26.6 us  [local(): mine = lax.all_to_all(block, 'tmpl', 0, 0).reshape(-1, share)]
    all_to_all x1 -> x0, waiting for transfers between devices: 14.5 us -> none  [local(): mine = lax.all_to_all(block, 'tmpl', 0, 0).reshape(-1, share)]
    all_to_all x1 -> x0, starting transfers between devices: 11.2 us -> none  [local(): mine = lax.all_to_all(block, 'tmpl', 0, 0).reshape(-1, share)]
    unnamed x12, local copies, waits for them, and re-layouts: 2.49 us -> 0.03 us
    pallas_call x1, Pallas kernels: 1.5 us -> 0.61 us  [basis_share(): pl.pallas_call(last_kernel, out_shape=jax.ShapeDtypeStruct((chips, own.sh...]
    pallas_call x1, Pallas kernels: 3.25 us -> 2.38 us  [residual_of(): pl.pallas_call(functools.partial(residual_kernel, half), out_shape=(jax.S...]
    ppermute x1 -> x2, waiting for transfers between devices: 0.01 us -> 0.73 us  [the longest x1 0.73 us: local(): other_narrow = lax.ppermute(sent_narrow, 'sect', swap)]
    ppermute x1 -> x2, starting transfers between devices: 1.85 us -> 1.76 us  [the longest x1 1.64 us: local(): other_wide = lax.ppermute(sent_wide, 'sect', swap)]
  transfers between devices with their start and end apart: 5 -> 5, of which waited for: 2 -> 1; matrix products, arithmetic and copies ran while one was open for 0% -> 0% of each run, Pallas kernels for 7% -> 9%
where the time goes in v4:
time: 37.9 us; the launch traced here: 37.6 us
  blocking collectives  26.6 us (70%)
  Pallas kernels  5.8 us (15%)
  starting transfers between devices  3.73 us (10%)
  waiting for transfers between devices  0.74 us (2%)
  between operations  0.73 us (2%)
    all_to_all x1, blocking collectives, local(): mine = lax.all_to_all(block, 'tmpl', 0, 0).reshape(-1, share)  26.6 us
    pallas_call x1, Pallas kernels, residual_of(): pl.pallas_call(functools.partial(residual_kernel, half), out_shape=(jax.S...  2.38 us
    ppermute x1, starting transfers between devices, local(): other_wide = lax.ppermute(sent_wide, 'sect', swap)  1.64 us
    ppermute x1, starting transfers between devices, local(): other_line = lax.ppermute(strain, 'sect', swap)  1.46 us
    pallas_call x1, Pallas kernels, first_columns(): pl.pallas_call(first_kernel, in_specs=[pl.BlockSpec(memory_space=pltpu.HB...  1.19 us
    pallas_call x2, Pallas kernels, partial_products(): pl.pallas_call(kernel, out_shape=(jax.ShapeDtypeStruct((columns, count),...  0.86 us
  transfers between devices with their start and end apart: 5, of which 1 were waited for; matrix products, arithmetic and copies ran while one was open for 0% of the time, Pallas kernels for 9%

profile of v4, /device:TPU:1, one launch (start us, length us, event | category | flops | bytes accessed | tf_op | source)
XLA Modules:
  0.0 37.6 jit_solution(3240960385370424963)
XLA Ops:
  0.6 1.5 %collective-permute-start = (bf16[1,1535]{1,0:T(2,128)(2,1)}, bf16[1,1535]{1,0:T(2,128)(2,1)S(1)}, u32[]{:S(2)}, u32[]{:S(2)}) collective-permute-start(bf16[1,1535]{1,0:T(2,128)(2,1)} %own_line_ref.1), channel_id=1, source_target_pairs={{0,64},{64,0},{1,65},{65,1},{2,66},{66,2},{3,67},{67,3},{4,68},{68... | collective-permute-start | bytes 9218 | tf_op jit(solution)/shard_map/ppermute | solution.py:315
  2.1 0.1 collective-permute-start.1
  2.2 0.0 copy-start.3
  2.2 0.0 copy-start.4
  2.2 0.4 %collective-permute-start.2 = (bf16[512,1024]{1,0:T(8,128)(2,1)}, bf16[512,1024]{1,0:T(8,128)(2,1)S(1)}, u32[]{:S(2)}, u32[]{:S(2)}) collective-permute-start(bf16[512,1024]{1,0:T(8,128)(2,1)} %bitcast.12), channel_id=1, source_target_pairs={{0,64},{64,0},{1,65},{65,1},{2,66},{66,2},{3,67},{67,3},{4,68},{68... | collective-permute-start | bytes 3145736 | tf_op jit(solution)/shard_map/ppermute | solution.py:317
  2.6 1.2 %first_columns.1.first_ref = bf16[16,256]{1,0:T(8,128)(2,1)S(1)} custom-call(bf16[1,1535]{1,0:T(2,128)(2,1)} %own_line_ref.1, bf16[16,1024]{1,0:T(8,128)(2,1)} %bitcast.16), custom_call_target="tpu_custom_call" | custom-call | flops 1073741824 | bytes 4194304 | tf_op jit(solution)/shard_map/first_columns/pallas_call | solution.py:67
  3.8 0.0 copy-start
  3.8 0.0 collective-permute-done.other_line_ref
  3.8 0.0 collective-permute-done.1.other_ref
  3.8 0.0 copy-done.3
  3.8 0.0 copy-done.4
  3.9 0.6 %basis_share.1 = bf16[64,16,384]{2,1,0:T(8,128)(2,1)S(1)} custom-call(bf16[1,1535]{1,0:T(2,128)(2,1)S(1)} %copy-done.4, bf16[1,1535]{1,0:T(2,128)(2,1)S(1)} %collective-permute-done.other_line_ref, bf16[16,1024]{1,0:T(8,128)(2,1)S(1)} %bitcast.17, bf16[16,1024]{1,0:T(8,128)(2,1)S(1)} %collective-permute-done.1.other_ref, ...), custom_call_target="tpu_custom_call" | custom-call | tf_op jit(solution)/shard_map/basis_share/pallas_call | solution.py:103
  4.5 26.6 %all_to_all.5 = bf16[64,16,384]{2,1,0:T(8,128)(2,1)S(1)} all-to-all(bf16[64,16,384]{2,1,0:T(8,128)(2,1)S(1)} %basis_share.1), channel_id=1, replica_groups=mesh['sect'=2,'tmpl'=64] {'tmpl'}, dimensions={0} | all-to-all | bytes 1572864 | tf_op jit(solution)/shard_map/all_to_all | solution.py:320
  31.0 0.0 copy-done
  31.0 0.4 %shard_map.77 = (f32[512,256]{1,0:T(8,128)S(1)}, f32[512,256]{1,0:T(8,128)S(1)}) custom-call(bf16[512,1024]{1,0:T(8,128)(2,1)S(1)} %bitcast.13, bf16[1024,384]{1,0:T(8,128)(2,1)S(1)} %bitcast.10), custom_call_target="tpu_custom_call" | custom-call | flops 536870912 | bytes 2097152 | tf_op jit(solution)/shard_map/pallas_call | solution.py:148
  31.5 0.0 copy-start.1
  31.5 0.0 copy-start.5
  31.5 1.6 %collective-permute-start.3 = (f32[512,256]{1,0:T(8,128)S(1)}, f32[512,256]{1,0:T(8,128)S(1)}, u32[]{:S(2)}, u32[]{:S(2)}) collective-permute-start(f32[512,256]{1,0:T(8,128)S(1)} %get-tuple-element.10), channel_id=1, source_target_pairs={{0,64},{64,0},{1,65},{65,1},{2,66},{66,2},{3,67},{67,3},{4,68},{68... | collective-permute-start | bytes 1572872 | tf_op jit(solution)/shard_map/ppermute | solution.py:322
  33.2 0.0 collective-permute-done.2.other_ref
  33.2 0.4 %shard_map.78 = (f32[512,128]{1,0:T(8,128)S(1)}, f32[512,128]{1,0:T(8,128)S(1)}) custom-call(bf16[512,1024]{1,0:T(8,128)(2,1)S(1)} %bitcast.14, bf16[512,1024]{1,0:T(8,128)(2,1)S(1)} %collective-permute-done.2.other_ref, bf16[1024,384]{1,0:T(8,128)(2,1)S(1)} %bitcast.11), custom_call_target="tpu_custom_call" | custom-call | flops 536870912 | bytes 2097152 | tf_op jit(solution)/shard_map/pallas_call | solution.py:148
  33.6 0.1 collective-permute-start.4
  33.7 0.0 copy-done.1
  33.7 0.0 copy-done.5
  33.7 0.0 copy-start.2
  33.7 0.8 %lag_spectrum.1 = (f32[512,768]{1,0:T(8,128)S(1)}, f32[256,128]{1,0:T(8,128)S(1)}) custom-call(f32[351,4,128]{2,1,0:T(4,128)S(1)} %bitcast.18, bf16[512,768]{1,0:T(8,128)(2,1)S(1)} %copy-done.1), custom_call_target="tpu_custom_call" | custom-call | flops 1073741824 | bytes 4194304 | tf_op jit(solution)/shard_map/lag_spectrum/pallas_call | solution.py:187
  34.5 0.7 %collective-permute-done.4.other_narrow_ref = f32[512,128]{1,0:T(8,128)S(1)} collective-permute-done((f32[512,128]{1,0:T(8,128)S(1)}, f32[512,128]{1,0:T(8,128)S(1)}, u32[]{:S(2)}, u32[]{:S(2)}) %collective-permute-start.4) | collective-permute-done | bytes 262176 | tf_op jit(solution)/shard_map/ppermute | solution.py:324
  35.2 0.0 collective-permute-done.3.other_wide_ref
  35.2 0.0 copy-done.2
  35.2 2.4 %residual.1 = (bf16[512,256]{1,0:T(8,128)(2,1)}, f32[256,256]{1,0:T(8,128)}) custom-call(f32[512,256]{1,0:T(8,128)S(1)} %get-tuple-element.8.own_wide_ref, f32[512,128]{1,0:T(8,128)S(1)} %get-tuple-element.9.own_narrow_ref, f32[512,256]{1,0:T(8,128)S(1)} %collective-permute-done.3.other_wide_ref, f32[512,128]{1,0:T(8,128)S(1)} %collective-permute-done.4.other_narrow_ref, ...), custom_call_target="tpu_custom_call" | custom-call | tf_op jit(solution)/shard_map/residual/pallas_call | solution.py:291
Async XLA Ops:
  0.6 3.2 %collective-permute-start = (bf16[1,1535]{1,0:T(2,128)(2,1)}, bf16[1,1535]{1,0:T(2,128)(2,1)S(1)}, u32[]{:S(2)}, u32[]{:S(2)}) collective-permute-start(bf16[1,1535]{1,0:T(2,128)(2,1)} %own_line_ref.1), channel_id=1, source_target_pairs={{0,64},{64,0},{1,65},{65,1},{2,66},{66,2},{3,67},{67,3},{4,68},{68... | collective-permute-start | bytes 9218 | tf_op jit(solution)/shard_map/ppermute | solution.py:315
  2.1 1.7 %collective-permute-start.1 = (bf16[16,1024]{1,0:T(8,128)(2,1)}, bf16[16,1024]{1,0:T(8,128)(2,1)S(1)}, u32[]{:S(2)}, u32[]{:S(2)}) collective-permute-start(bf16[16,1024]{1,0:T(8,128)(2,1)} %bitcast.15), channel_id=1, source_target_pairs={{0,64},{64,0},{1,65},{65,1},{2,66},{66,2},{3,67},{67,3},{4,68},{68... | collective-permute-start | bytes 98312 | tf_op jit(solution)/shard_map/ppermute | solution.py:316
  2.2 1.7 %copy-start.3 = (bf16[1,16,1024]{2,1,0:T(8,128)(2,1)S(1)}, bf16[1,16,1024]{2,1,0:T(8,128)(2,1)}, u32[]{:S(2)}) copy-start(bf16[1,16,1024]{2,1,0:T(8,128)(2,1)} %param.7) | copy-start | bytes 98308
  2.2 1.7 %copy-start.4 = (bf16[1,1535]{1,0:T(2,128)(2,1)S(1)}, bf16[1,1535]{1,0:T(2,128)(2,1)}, u32[]{:S(2)}) copy-start(bf16[1,1535]{1,0:T(2,128)(2,1)} %own_line_ref.1) | copy-start | bytes 9214
  2.2 31.0 %collective-permute-start.2 = (bf16[512,1024]{1,0:T(8,128)(2,1)}, bf16[512,1024]{1,0:T(8,128)(2,1)S(1)}, u32[]{:S(2)}, u32[]{:S(2)}) collective-permute-start(bf16[512,1024]{1,0:T(8,128)(2,1)} %bitcast.12), channel_id=1, source_target_pairs={{0,64},{64,0},{1,65},{65,1},{2,66},{66,2},{3,67},{67,3},{4,68},{68... | collective-permute-start | bytes 3145736 | tf_op jit(solution)/shard_map/ppermute | solution.py:317
  3.8 27.2 %copy-start = (bf16[1,512,1024]{2,1,0:T(8,128)(2,1)S(1)}, bf16[1,512,1024]{2,1,0:T(8,128)(2,1)}, u32[]{:S(2)}) copy-start(bf16[1,512,1024]{2,1,0:T(8,128)(2,1)} %param.8) | copy-start | bytes 3145732
  31.5 2.2 %copy-start.1 = (bf16[512,768]{1,0:T(8,128)(2,1)S(1)}, bf16[512,768]{1,0:T(8,128)(2,1)}, u32[]{:S(2)}) copy-start(bf16[512,768]{1,0:T(8,128)(2,1)} %constant.4.clone.forward_ref) | copy-start | bytes 2359300
  31.5 2.2 %copy-start.5 = (f32[256,2,351]{0,1,2:T(2,128)S(1)}, f32[256,2,351]{0,1,2:T(2,128)}, u32[]{:S(2)}) copy-start(f32[256,2,351]{0,1,2:T(2,128)} %param.9) | copy-start | bytes 2156548
  31.5 3.7 %collective-permute-start.3 = (f32[512,256]{1,0:T(8,128)S(1)}, f32[512,256]{1,0:T(8,128)S(1)}, u32[]{:S(2)}, u32[]{:S(2)}) collective-permute-start(f32[512,256]{1,0:T(8,128)S(1)} %get-tuple-element.10), channel_id=1, source_target_pairs={{0,64},{64,0},{1,65},{65,1},{2,66},{66,2},{3,67},{67,3},{4,68},{68... | collective-permute-start | bytes 1572872 | tf_op jit(solution)/shard_map/ppermute | solution.py:322
  33.6 1.6 %collective-permute-start.4 = (f32[512,128]{1,0:T(8,128)S(1)}, f32[512,128]{1,0:T(8,128)S(1)}, u32[]{:S(2)}, u32[]{:S(2)}) collective-permute-start(f32[512,128]{1,0:T(8,128)S(1)} %get-tuple-element.11), channel_id=1, source_target_pairs={{0,64},{64,0},{1,65},{65,1},{2,66},{66,2},{3,67},{67,3},{4,68},{68... | collective-permute-start | bytes 786440 | tf_op jit(solution)/shard_map/ppermute | solution.py:324
  33.7 1.5 %copy-start.2 = (bf16[768,512]{1,0:T(8,128)(2,1)S(1)}, bf16[768,512]{1,0:T(8,128)(2,1)}, u32[]{:S(2)}) copy-start(bf16[768,512]{1,0:T(8,128)(2,1)} %constant.5.clone.inverse_ref) | copy-start | bytes 2359300

commit v5 on v4

--- a/solution.py
+++ b/solution.py
@@ -37,11 +37,12 @@
     spread = jnp.broadcast_to(line, (rows, width))
     shifted = pltpu.roll(spread, width - (rows - 1), 1, stride=1, stride_axis=0).astype(jnp.bfloat16)
     total = jnp.zeros((bank.shape[0], count), jnp.float32)
-    for start in range(0, taps, rows):
-        part = jnp.dot(bank[:, start : start + rows], flip, preferred_element_type=jnp.float32)
-        total += jnp.dot(
-            part.astype(jnp.bfloat16), shifted[:, start : start + count], preferred_element_type=jnp.float32
-        )
+    starts = range(0, taps, rows)
+    stacked = jnp.concatenate([bank[:, start : start + rows] for start in starts], axis=0)
+    turned = jnp.dot(stacked, flip, preferred_element_type=jnp.float32).astype(jnp.bfloat16)
+    for step, start in enumerate(starts):
+        part = turned[step * bank.shape[0] : (step + 1) * bank.shape[0]]
+        total += jnp.dot(part, shifted[:, start : start + count], preferred_element_type=jnp.float32)
     return total.astype(jnp.bfloat16)
 
 

time: 37.9 us -> 37.6 us (level)
  transfers between devices with their start and end apart: 5 -> 5, of which waited for: 1 -> 1; matrix products, arithmetic and copies ran while one was open for 0% -> 0% of each run, Pallas kernels for 9% -> 8%
where the time goes in v5:
time: 37.6 us; the launch traced here: 37.3 us
  blocking collectives  26.6 us (71%)
  Pallas kernels  5.48 us (15%)
  starting transfers between devices  3.72 us (10%)
  waiting for transfers between devices  0.74 us (2%)
  between operations  0.73 us (2%)
    all_to_all x1, blocking collectives, local(): mine = lax.all_to_all(block, 'tmpl', 0, 0).reshape(-1, share)  26.6 us
    pallas_call x1, Pallas kernels, residual_of(): pl.pallas_call(functools.partial(residual_kernel, half), out_shape=(jax.S...  2.38 us
    ppermute x1, starting transfers between devices, local(): other_wide = lax.ppermute(sent_wide, 'sect', swap)  1.64 us
    ppermute x1, starting transfers between devices, local(): other_line = lax.ppermute(strain, 'sect', swap)  1.46 us
    pallas_call x1, Pallas kernels, first_columns(): pl.pallas_call(first_kernel, in_specs=[pl.BlockSpec(memory_space=pltpu.HB...  1.14 us
    pallas_call x2, Pallas kernels, partial_products(): pl.pallas_call(kernel, out_shape=(jax.ShapeDtypeStruct((columns, count),...  0.87 us
  transfers between devices with their start and end apart: 5, of which 1 were waited for; matrix products, arithmetic and copies ran while one was open for 0% of the time, Pallas kernels for 8%

profile of v5, /device:TPU:1, one launch (start us, length us, event | category | flops | bytes accessed | tf_op | source)
XLA Modules:
  0.0 37.3 jit_solution(16897921742650522404)
XLA Ops:
  0.6 1.5 %collective-permute-start = (bf16[1,1535]{1,0:T(2,128)(2,1)}, bf16[1,1535]{1,0:T(2,128)(2,1)S(1)}, u32[]{:S(2)}, u32[]{:S(2)}) collective-permute-start(bf16[1,1535]{1,0:T(2,128)(2,1)} %own_line_ref.1), channel_id=1, source_target_pairs={{0,64},{64,0},{1,65},{65,1},{2,66},{66,2},{3,67},{67,3},{4,68},{68... | collective-permute-start | bytes 9218 | tf_op jit(solution)/shard_map/ppermute | solution.py:316
  2.1 0.1 collective-permute-start.1
  2.2 0.0 copy-start.3
  2.2 0.0 copy-start.4
  2.2 0.4 %collective-permute-start.2 = (bf16[512,1024]{1,0:T(8,128)(2,1)}, bf16[512,1024]{1,0:T(8,128)(2,1)S(1)}, u32[]{:S(2)}, u32[]{:S(2)}) collective-permute-start(bf16[512,1024]{1,0:T(8,128)(2,1)} %bitcast.12), channel_id=1, source_target_pairs={{0,64},{64,0},{1,65},{65,1},{2,66},{66,2},{3,67},{67,3},{4,68},{68... | collective-permute-start | bytes 3145736 | tf_op jit(solution)/shard_map/ppermute | solution.py:318
  2.6 1.1 %first_columns.1.first_ref = bf16[16,256]{1,0:T(8,128)(2,1)S(1)} custom-call(bf16[1,1535]{1,0:T(2,128)(2,1)} %own_line_ref.1, bf16[16,1024]{1,0:T(8,128)(2,1)} %bitcast.16), custom_call_target="tpu_custom_call" | custom-call | flops 1073741824 | bytes 4194304 | tf_op jit(solution)/shard_map/first_columns/pallas_call | solution.py:68
  3.8 0.0 copy-start
  3.8 0.0 collective-permute-done.other_line_ref
  3.8 0.0 collective-permute-done.1.other_ref
  3.8 0.0 copy-done.3
  3.8 0.0 copy-done.4
  3.8 0.3 basis_share.1
  4.2 26.6 %all_to_all.5 = bf16[64,16,384]{2,1,0:T(8,128)(2,1)S(1)} all-to-all(bf16[64,16,384]{2,1,0:T(8,128)(2,1)S(1)} %basis_share.1), channel_id=1, replica_groups=mesh['sect'=2,'tmpl'=64] {'tmpl'}, dimensions={0} | all-to-all | bytes 1572864 | tf_op jit(solution)/shard_map/all_to_all | solution.py:321
  30.7 0.0 copy-done
  30.7 0.4 %shard_map.77 = (f32[512,256]{1,0:T(8,128)S(1)}, f32[512,256]{1,0:T(8,128)S(1)}) custom-call(bf16[512,1024]{1,0:T(8,128)(2,1)S(1)} %bitcast.13, bf16[1024,384]{1,0:T(8,128)(2,1)S(1)} %bitcast.10), custom_call_target="tpu_custom_call" | custom-call | flops 536870912 | bytes 2097152 | tf_op jit(solution)/shard_map/pallas_call | solution.py:149
  31.2 0.0 copy-start.1
  31.2 0.0 copy-start.5
  31.2 1.6 %collective-permute-start.3 = (f32[512,256]{1,0:T(8,128)S(1)}, f32[512,256]{1,0:T(8,128)S(1)}, u32[]{:S(2)}, u32[]{:S(2)}) collective-permute-start(f32[512,256]{1,0:T(8,128)S(1)} %get-tuple-element.10), channel_id=1, source_target_pairs={{0,64},{64,0},{1,65},{65,1},{2,66},{66,2},{3,67},{67,3},{4,68},{68... | collective-permute-start | bytes 1572872 | tf_op jit(solution)/shard_map/ppermute | solution.py:323
  32.8 0.0 collective-permute-done.2.other_ref
  32.8 0.4 %shard_map.78 = (f32[512,128]{1,0:T(8,128)S(1)}, f32[512,128]{1,0:T(8,128)S(1)}) custom-call(bf16[512,1024]{1,0:T(8,128)(2,1)S(1)} %bitcast.14, bf16[512,1024]{1,0:T(8,128)(2,1)S(1)} %collective-permute-done.2.other_ref, bf16[1024,384]{1,0:T(8,128)(2,1)S(1)} %bitcast.11), custom_call_target="tpu_custom_call" | custom-call | flops 536870912 | bytes 2097152 | tf_op jit(solution)/shard_map/pallas_call | solution.py:149
  33.3 0.1 collective-permute-start.4
  33.4 0.0 copy-done.1
  33.4 0.0 copy-done.5
  33.4 0.0 copy-start.2
  33.4 0.7 %lag_spectrum.1 = (f32[512,768]{1,0:T(8,128)S(1)}, f32[256,128]{1,0:T(8,128)S(1)}) custom-call(f32[351,4,128]{2,1,0:T(4,128)S(1)} %bitcast.18, bf16[512,768]{1,0:T(8,128)(2,1)S(1)} %copy-done.1), custom_call_target="tpu_custom_call" | custom-call | flops 1073741824 | bytes 4194304 | tf_op jit(solution)/shard_map/lag_spectrum/pallas_call | solution.py:188
  34.2 0.7 %collective-permute-done.4.other_narrow_ref = f32[512,128]{1,0:T(8,128)S(1)} collective-permute-done((f32[512,128]{1,0:T(8,128)S(1)}, f32[512,128]{1,0:T(8,128)S(1)}, u32[]{:S(2)}, u32[]{:S(2)}) %collective-permute-start.4) | collective-permute-done | bytes 262176 | tf_op jit(solution)/shard_map/ppermute | solution.py:325
  34.9 0.0 collective-permute-done.3.other_wide_ref
  34.9 0.0 copy-done.2
  34.9 2.4 %residual.1 = (bf16[512,256]{1,0:T(8,128)(2,1)}, f32[256,256]{1,0:T(8,128)}) custom-call(f32[512,256]{1,0:T(8,128)S(1)} %get-tuple-element.8.own_wide_ref, f32[512,128]{1,0:T(8,128)S(1)} %get-tuple-element.9.own_narrow_ref, f32[512,256]{1,0:T(8,128)S(1)} %collective-permute-done.3.other_wide_ref, f32[512,128]{1,0:T(8,128)S(1)} %collective-permute-done.4.other_narrow_ref, ...), custom_call_target="tpu_custom_call" | custom-call | tf_op jit(solution)/shard_map/residual/pallas_call | solution.py:292
Async XLA Ops:
  0.6 3.1 %collective-permute-start = (bf16[1,1535]{1,0:T(2,128)(2,1)}, bf16[1,1535]{1,0:T(2,128)(2,1)S(1)}, u32[]{:S(2)}, u32[]{:S(2)}) collective-permute-start(bf16[1,1535]{1,0:T(2,128)(2,1)} %own_line_ref.1), channel_id=1, source_target_pairs={{0,64},{64,0},{1,65},{65,1},{2,66},{66,2},{3,67},{67,3},{4,68},{68... | collective-permute-start | bytes 9218 | tf_op jit(solution)/shard_map/ppermute | solution.py:316
  2.1 1.7 %collective-permute-start.1 = (bf16[16,1024]{1,0:T(8,128)(2,1)}, bf16[16,1024]{1,0:T(8,128)(2,1)S(1)}, u32[]{:S(2)}, u32[]{:S(2)}) collective-permute-start(bf16[16,1024]{1,0:T(8,128)(2,1)} %bitcast.15), channel_id=1, source_target_pairs={{0,64},{64,0},{1,65},{65,1},{2,66},{66,2},{3,67},{67,3},{4,68},{68... | collective-permute-start | bytes 98312 | tf_op jit(solution)/shard_map/ppermute | solution.py:317
  2.2 1.6 %copy-start.3 = (bf16[1,16,1024]{2,1,0:T(8,128)(2,1)S(1)}, bf16[1,16,1024]{2,1,0:T(8,128)(2,1)}, u32[]{:S(2)}) copy-start(bf16[1,16,1024]{2,1,0:T(8,128)(2,1)} %param.7) | copy-start | bytes 98308
  2.2 1.6 %copy-start.4 = (bf16[1,1535]{1,0:T(2,128)(2,1)S(1)}, bf16[1,1535]{1,0:T(2,128)(2,1)}, u32[]{:S(2)}) copy-start(bf16[1,1535]{1,0:T(2,128)(2,1)} %own_line_ref.1) | copy-start | bytes 9214
  2.2 30.7 %collective-permute-start.2 = (bf16[512,1024]{1,0:T(8,128)(2,1)}, bf16[512,1024]{1,0:T(8,128)(2,1)S(1)}, u32[]{:S(2)}, u32[]{:S(2)}) collective-permute-start(bf16[512,1024]{1,0:T(8,128)(2,1)} %bitcast.12), channel_id=1, source_target_pairs={{0,64},{64,0},{1,65},{65,1},{2,66},{66,2},{3,67},{67,3},{4,68},{68... | collective-permute-start | bytes 3145736 | tf_op jit(solution)/shard_map/ppermute | solution.py:318
  3.8 27.0 %copy-start = (bf16[1,512,1024]{2,1,0:T(8,128)(2,1)S(1)}, bf16[1,512,1024]{2,1,0:T(8,128)(2,1)}, u32[]{:S(2)}) copy-start(bf16[1,512,1024]{2,1,0:T(8,128)(2,1)} %param.8) | copy-start | bytes 3145732
  31.2 2.2 %copy-start.1 = (bf16[512,768]{1,0:T(8,128)(2,1)S(1)}, bf16[512,768]{1,0:T(8,128)(2,1)}, u32[]{:S(2)}) copy-start(bf16[512,768]{1,0:T(8,128)(2,1)} %constant.4.clone.forward_ref) | copy-start | bytes 2359300
  31.2 2.2 %copy-start.5 = (f32[256,2,351]{0,1,2:T(2,128)S(1)}, f32[256,2,351]{0,1,2:T(2,128)}, u32[]{:S(2)}) copy-start(f32[256,2,351]{0,1,2:T(2,128)} %param.9) | copy-start | bytes 2156548
  31.2 3.7 %collective-permute-start.3 = (f32[512,256]{1,0:T(8,128)S(1)}, f32[512,256]{1,0:T(8,128)S(1)}, u32[]{:S(2)}, u32[]{:S(2)}) collective-permute-start(f32[512,256]{1,0:T(8,128)S(1)} %get-tuple-element.10), channel_id=1, source_target_pairs={{0,64},{64,0},{1,65},{65,1},{2,66},{66,2},{3,67},{67,3},{4,68},{68... | collective-permute-start | bytes 1572872 | tf_op jit(solution)/shard_map/ppermute | solution.py:323
  33.3 1.6 %collective-permute-start.4 = (f32[512,128]{1,0:T(8,128)S(1)}, f32[512,128]{1,0:T(8,128)S(1)}, u32[]{:S(2)}, u32[]{:S(2)}) collective-permute-start(f32[512,128]{1,0:T(8,128)S(1)} %get-tuple-element.11), channel_id=1, source_target_pairs={{0,64},{64,0},{1,65},{65,1},{2,66},{66,2},{3,67},{67,3},{4,68},{68... | collective-permute-start | bytes 786440 | tf_op jit(solution)/shard_map/ppermute | solution.py:325
  33.4 1.5 %copy-start.2 = (bf16[768,512]{1,0:T(8,128)(2,1)S(1)}, bf16[768,512]{1,0:T(8,128)(2,1)}, u32[]{:S(2)}) copy-start(bf16[768,512]{1,0:T(8,128)(2,1)} %constant.5.clone.inverse_ref) | copy-start | bytes 2359300

commit v6 on v5

--- a/solution.py
+++ b/solution.py
@@ -13,7 +13,6 @@
 BINS = 384
 LANES = 128
 GRANT = 24 << 20
-SENT = jnp.float32
 
 
 def forward_matrix(rows):
@@ -27,18 +26,25 @@
     return np.concatenate([share * np.cos(angle), -share * np.sin(angle)], axis=0)
 
 
-def convolved(line, bank, count):
-    rows = 256
-    taps = bank.shape[1]
+ROWS = 256
+
+
+def flip_matrix():
+    row = lax.broadcasted_iota(jnp.int32, (ROWS, ROWS), 0)
+    col = lax.broadcasted_iota(jnp.int32, (ROWS, ROWS), 1)
+    return (row + col == ROWS - 1).astype(jnp.float32).astype(jnp.bfloat16)
+
+
+def toeplitz(line):
     width = line.shape[1]
-    row = lax.broadcasted_iota(jnp.int32, (rows, rows), 0)
-    col = lax.broadcasted_iota(jnp.int32, (rows, rows), 1)
-    flip = (row + col == rows - 1).astype(jnp.float32).astype(jnp.bfloat16)
-    spread = jnp.broadcast_to(line, (rows, width))
-    shifted = pltpu.roll(spread, width - (rows - 1), 1, stride=1, stride_axis=0).astype(jnp.bfloat16)
+    spread = jnp.broadcast_to(line, (ROWS, width))
+    return pltpu.roll(spread, width - (ROWS - 1), 1, stride=1, stride_axis=0).astype(jnp.bfloat16)
+
+
+def convolved(shifted, flip, bank, count):
     total = jnp.zeros((bank.shape[0], count), jnp.float32)
-    starts = range(0, taps, rows)
-    stacked = jnp.concatenate([bank[:, start : start + rows] for start in starts], axis=0)
+    starts = range(0, bank.shape[1], ROWS)
+    stacked = jnp.concatenate([bank[:, start : start + ROWS] for start in starts], axis=0)
     turned = jnp.dot(stacked, flip, preferred_element_type=jnp.float32).astype(jnp.bfloat16)
     for step, start in enumerate(starts):
         part = turned[step * bank.shape[0] : (step + 1) * bank.shape[0]]
@@ -54,13 +60,14 @@
     bank_copy = pltpu.make_async_copy(bank_hbm, bank_ref, sems.at[1])
     line_copy.start()
     bank_copy.start()
+    line_ref[...] = jnp.zeros_like(line_ref)
+    flip = flip_matrix()
     line_copy.wait()
-    line_ref[...] = jnp.zeros_like(line_ref)
     line_ref[0:1, 0 : raw_ref.shape[1]] = raw_ref[...].astype(jnp.float32)
     begin = pl.multiple_of(section * LANES, LANES)
+    bank_copy.wait()
     line = line_ref[0:1, pl.ds(begin, taps + wide)]
-    bank_copy.wait()
-    basis_ref[...] = convolved(line, bank_ref[...], wide)
+    basis_ref[...] = convolved(toeplitz(line), flip, bank_ref[...], wide)
 
 
 def first_columns(line, bank, wide):
@@ -92,7 +99,7 @@
     own = line_ref[0:1, share : share + taps + LANES]
     line = jnp.where(section == 0, line_ref[8:9, 0 : taps + LANES], own)
     bank = jnp.where(section == 0, other_ref[...].astype(jnp.float32), own_ref[...].astype(jnp.float32))
-    last = convolved(line, bank.astype(jnp.bfloat16), LANES)
+    last = convolved(toeplitz(line), flip_matrix(), bank.astype(jnp.bfloat16), LANES)
     basis = jnp.concatenate([first_ref[...], last], axis=1)
     for chip in range(basis_ref.shape[0]):
         basis_ref[chip] = basis
@@ -119,21 +126,17 @@
     return lax.dot_general(left, right, (((0,), (0,)), ((), ())), preferred_element_type=jnp.float32)
 
 
-def wide_kernel(own_ref, basis_ref, kept_ref, sent_ref):
-    wide = kept_ref.shape[1]
-    value = jnp.dot(own_ref[...], basis_ref[:, 0:wide], preferred_element_type=jnp.float32)
-    kept_ref[...] = value
-    sent_ref[...] = value.astype(sent_ref.dtype)
-
-
-def narrow_kernel(own_ref, other_ref, basis_ref, kept_ref, sent_ref):
+def wide_kernel(own_ref, basis_ref, part_ref):
+    wide = part_ref.shape[1]
+    part_ref[...] = jnp.dot(own_ref[...], basis_ref[:, 0:wide], preferred_element_type=jnp.float32)
+
+
+def narrow_kernel(own_ref, other_ref, basis_ref, part_ref):
     section = lax.axis_index("sect")
     wide = basis_ref.shape[1] - LANES
 
     def multiply(fast_ref):
-        value = jnp.dot(fast_ref[...], basis_ref[:, wide:], preferred_element_type=jnp.float32)
-        kept_ref[...] = value
-        sent_ref[...] = value.astype(sent_ref.dtype)
+        part_ref[...] = jnp.dot(fast_ref[...], basis_ref[:, wide:], preferred_element_type=jnp.float32)
 
     @pl.when(section == 0)
     def _():
@@ -148,10 +151,7 @@
     columns = operands[0].shape[0]
     return pl.pallas_call(
         kernel,
-        out_shape=(
-            jax.ShapeDtypeStruct((columns, count), jnp.float32),
-            jax.ShapeDtypeStruct((columns, count), SENT),
-        ),
+        out_shape=jax.ShapeDtypeStruct((columns, count), jnp.float32),
         compiler_params=pltpu.CompilerParams(vmem_limit_bytes=GRANT),
         cost_estimate=pl.CostEstimate(flops=1 << 29, bytes_accessed=1 << 21, transcendentals=0),
     )(*operands)
@@ -319,10 +319,10 @@
     first = first_columns(strain, own_bank, share - LANES)
     block = basis_share(strain, other_line, own_bank, other_bank, first, chips)
     mine = lax.all_to_all(block, "tmpl", 0, 0).reshape(-1, share)
-    own_wide, sent_wide = partial_products(wide_kernel, share - LANES, own_rows, mine)
-    other_wide = lax.ppermute(sent_wide, "sect", swap)
-    own_narrow, sent_narrow = partial_products(narrow_kernel, LANES, own_rows, other_rows, mine)
-    other_narrow = lax.ppermute(sent_narrow, "sect", swap)
+    own_wide = partial_products(wide_kernel, share - LANES, own_rows, mine)
+    other_wide = lax.ppermute(own_wide, "sect", swap)
+    own_narrow = partial_products(narrow_kernel, LANES, own_rows, other_rows, mine)
+    other_narrow = lax.ppermute(own_narrow, "sect", swap)
     spectrum, weight = lag_spectrum(correlation, forward)
     pieces = (own_wide, own_narrow, other_wide, other_narrow)
     return residual_of(pieces, spectrum, weight, forward, inverse, half, samples // sections)

time: 37.6 us -> 37.6 us (level)
  no operation moved by 1% of the time
where the time goes in v6:
time: 37.6 us; the launch traced here: 37.3 us
  blocking collectives  26.6 us (71%)
  Pallas kernels  5.48 us (15%)
  starting transfers between devices  3.72 us (10%)
  waiting for transfers between devices  0.74 us (2%)
  between operations  0.73 us (2%)
    all_to_all x1, blocking collectives, local(): mine = lax.all_to_all(block, 'tmpl', 0, 0).reshape(-1, share)  26.6 us
    pallas_call x1, Pallas kernels, residual_of(): pl.pallas_call(functools.partial(residual_kernel, half), out_shape=(jax.S...  2.38 us
    ppermute x1, starting transfers between devices, local(): other_wide = lax.ppermute(own_wide, 'sect', swap)  1.64 us
    ppermute x1, starting transfers between devices, local(): other_line = lax.ppermute(strain, 'sect', swap)  1.46 us
    pallas_call x1, Pallas kernels, first_columns(): pl.pallas_call(first_kernel, in_specs=[pl.BlockSpec(memory_space=pltpu.HB...  1.13 us
    pallas_call x2, Pallas kernels, partial_products(): pl.pallas_call(kernel, out_shape=jax.ShapeDtypeStruct((columns, count), j...  0.87 us
  transfers between devices with their start and end apart: 5, of which 1 were waited for; matrix products, arithmetic and copies ran while one was open for 0% of the time, Pallas kernels for 8%

profile of v6, /device:TPU:1, one launch (start us, length us, event | category | flops | bytes accessed | tf_op | source)
XLA Modules:
  0.0 37.3 jit_solution(2520704103854082851)
XLA Ops:
  0.6 1.5 %collective-permute-start = (bf16[1,1535]{1,0:T(2,128)(2,1)}, bf16[1,1535]{1,0:T(2,128)(2,1)S(1)}, u32[]{:S(2)}, u32[]{:S(2)}) collective-permute-start(bf16[1,1535]{1,0:T(2,128)(2,1)} %own_line_ref.1), channel_id=1, source_target_pairs={{0,64},{64,0},{1,65},{65,1},{2,66},{66,2},{3,67},{67,3},{4,68},{68... | collective-permute-start | bytes 9218 | tf_op jit(solution)/shard_map/ppermute | solution.py:316
  2.1 0.1 collective-permute-start.1
  2.2 0.0 copy-start.3
  2.2 0.0 copy-start.4
  2.2 0.4 %collective-permute-start.2 = (bf16[512,1024]{1,0:T(8,128)(2,1)}, bf16[512,1024]{1,0:T(8,128)(2,1)S(1)}, u32[]{:S(2)}, u32[]{:S(2)}) collective-permute-start(bf16[512,1024]{1,0:T(8,128)(2,1)} %bitcast.12), channel_id=1, source_target_pairs={{0,64},{64,0},{1,65},{65,1},{2,66},{66,2},{3,67},{67,3},{4,68},{68... | collective-permute-start | bytes 3145736 | tf_op jit(solution)/shard_map/ppermute | solution.py:318
  2.6 1.1 %first_columns.1.first_ref = bf16[16,256]{1,0:T(8,128)(2,1)S(1)} custom-call(bf16[1,1535]{1,0:T(2,128)(2,1)} %own_line_ref.1, bf16[16,1024]{1,0:T(8,128)(2,1)} %bitcast.16), custom_call_target="tpu_custom_call" | custom-call | flops 1073741824 | bytes 4194304 | tf_op jit(solution)/shard_map/first_columns/pallas_call | solution.py:75
  3.7 0.0 copy-start
  3.8 0.0 collective-permute-done.other_line_ref
  3.8 0.0 collective-permute-done.1.other_ref
  3.8 0.0 copy-done.3
  3.8 0.0 copy-done.4
  3.8 0.3 basis_share.1
  4.2 26.6 %all_to_all.5 = bf16[64,16,384]{2,1,0:T(8,128)(2,1)S(1)} all-to-all(bf16[64,16,384]{2,1,0:T(8,128)(2,1)S(1)} %basis_share.1), channel_id=1, replica_groups=mesh['sect'=2,'tmpl'=64] {'tmpl'}, dimensions={0} | all-to-all | bytes 1572864 | tf_op jit(solution)/shard_map/all_to_all | solution.py:321
  30.7 0.0 copy-done
  30.7 0.4 %shard_map.77.own_wide_ref = f32[512,256]{1,0:T(8,128)S(1)} custom-call(bf16[512,1024]{1,0:T(8,128)(2,1)S(1)} %bitcast.13, bf16[1024,384]{1,0:T(8,128)(2,1)S(1)} %bitcast.10), custom_call_target="tpu_custom_call" | custom-call | flops 536870912 | bytes 2097152 | tf_op jit(solution)/shard_map/pallas_call | solution.py:152
  31.2 0.0 copy-start.1
  31.2 0.0 copy-start.5
  31.2 1.6 %collective-permute-start.3 = (f32[512,256]{1,0:T(8,128)S(1)}, f32[512,256]{1,0:T(8,128)S(1)}, u32[]{:S(2)}, u32[]{:S(2)}) collective-permute-start(f32[512,256]{1,0:T(8,128)S(1)} %shard_map.77.own_wide_ref), channel_id=1, source_target_pairs={{0,64},{64,0},{1,65},{65,1},{2,66},{66,2},{3,67},{67,3},{4,68},{68... | collective-permute-start | bytes 1572872 | tf_op jit(solution)/shard_map/ppermute | solution.py:323
  32.8 0.0 collective-permute-done.2.other_ref
  32.8 0.4 %shard_map.78.own_narrow_ref = f32[512,128]{1,0:T(8,128)S(1)} custom-call(bf16[512,1024]{1,0:T(8,128)(2,1)S(1)} %bitcast.14, bf16[512,1024]{1,0:T(8,128)(2,1)S(1)} %collective-permute-done.2.other_ref, bf16[1024,384]{1,0:T(8,128)(2,1)S(1)} %bitcast.11), custom_call_target="tpu_custom_call" | custom-call | flops 536870912 | bytes 2097152 | tf_op jit(solution)/shard_map/pallas_call | solution.py:152
  33.3 0.1 collective-permute-start.4
  33.4 0.0 copy-done.1
  33.4 0.0 copy-done.5
  33.4 0.0 copy-start.2
  33.4 0.8 %lag_spectrum.1 = (f32[512,768]{1,0:T(8,128)S(1)}, f32[256,128]{1,0:T(8,128)S(1)}) custom-call(f32[351,4,128]{2,1,0:T(4,128)S(1)} %bitcast.18, bf16[512,768]{1,0:T(8,128)(2,1)S(1)} %copy-done.1), custom_call_target="tpu_custom_call" | custom-call | flops 1073741824 | bytes 4194304 | tf_op jit(solution)/shard_map/lag_spectrum/pallas_call | solution.py:188
  34.2 0.7 %collective-permute-done.4.other_narrow_ref = f32[512,128]{1,0:T(8,128)S(1)} collective-permute-done((f32[512,128]{1,0:T(8,128)S(1)}, f32[512,128]{1,0:T(8,128)S(1)}, u32[]{:S(2)}, u32[]{:S(2)}) %collective-permute-start.4) | collective-permute-done | bytes 262176 | tf_op jit(solution)/shard_map/ppermute | solution.py:325
  34.9 0.0 collective-permute-done.3.other_wide_ref
  34.9 0.0 copy-done.2
  34.9 2.4 %residual.1 = (bf16[512,256]{1,0:T(8,128)(2,1)}, f32[256,256]{1,0:T(8,128)}) custom-call(f32[512,256]{1,0:T(8,128)S(1)} %shard_map.77.own_wide_ref, f32[512,128]{1,0:T(8,128)S(1)} %shard_map.78.own_narrow_ref, f32[512,256]{1,0:T(8,128)S(1)} %collective-permute-done.3.other_wide_ref, f32[512,128]{1,0:T(8,128)S(1)} %collective-permute-done.4.other_narrow_ref, ...), custom_call_target="tpu_custom_call" | custom-call | tf_op jit(solution)/shard_map/residual/pallas_call | solution.py:292
Async XLA Ops:
  0.6 3.1 %collective-permute-start = (bf16[1,1535]{1,0:T(2,128)(2,1)}, bf16[1,1535]{1,0:T(2,128)(2,1)S(1)}, u32[]{:S(2)}, u32[]{:S(2)}) collective-permute-start(bf16[1,1535]{1,0:T(2,128)(2,1)} %own_line_ref.1), channel_id=1, source_target_pairs={{0,64},{64,0},{1,65},{65,1},{2,66},{66,2},{3,67},{67,3},{4,68},{68... | collective-permute-start | bytes 9218 | tf_op jit(solution)/shard_map/ppermute | solution.py:316
  2.1 1.7 %collective-permute-start.1 = (bf16[16,1024]{1,0:T(8,128)(2,1)}, bf16[16,1024]{1,0:T(8,128)(2,1)S(1)}, u32[]{:S(2)}, u32[]{:S(2)}) collective-permute-start(bf16[16,1024]{1,0:T(8,128)(2,1)} %bitcast.15), channel_id=1, source_target_pairs={{0,64},{64,0},{1,65},{65,1},{2,66},{66,2},{3,67},{67,3},{4,68},{68... | collective-permute-start | bytes 98312 | tf_op jit(solution)/shard_map/ppermute | solution.py:317
  2.2 1.6 %copy-start.3 = (bf16[1,16,1024]{2,1,0:T(8,128)(2,1)S(1)}, bf16[1,16,1024]{2,1,0:T(8,128)(2,1)}, u32[]{:S(2)}) copy-start(bf16[1,16,1024]{2,1,0:T(8,128)(2,1)} %param.7) | copy-start | bytes 98308
  2.2 1.6 %copy-start.4 = (bf16[1,1535]{1,0:T(2,128)(2,1)S(1)}, bf16[1,1535]{1,0:T(2,128)(2,1)}, u32[]{:S(2)}) copy-start(bf16[1,1535]{1,0:T(2,128)(2,1)} %own_line_ref.1) | copy-start | bytes 9214
  2.2 30.7 %collective-permute-start.2 = (bf16[512,1024]{1,0:T(8,128)(2,1)}, bf16[512,1024]{1,0:T(8,128)(2,1)S(1)}, u32[]{:S(2)}, u32[]{:S(2)}) collective-permute-start(bf16[512,1024]{1,0:T(8,128)(2,1)} %bitcast.12), channel_id=1, source_target_pairs={{0,64},{64,0},{1,65},{65,1},{2,66},{66,2},{3,67},{67,3},{4,68},{68... | collective-permute-start | bytes 3145736 | tf_op jit(solution)/shard_map/ppermute | solution.py:318
  3.7 27.0 %copy-start = (bf16[1,512,1024]{2,1,0:T(8,128)(2,1)S(1)}, bf16[1,512,1024]{2,1,0:T(8,128)(2,1)}, u32[]{:S(2)}) copy-start(bf16[1,512,1024]{2,1,0:T(8,128)(2,1)} %param.8) | copy-start | bytes 3145732
  31.2 2.2 %copy-start.1 = (bf16[512,768]{1,0:T(8,128)(2,1)S(1)}, bf16[512,768]{1,0:T(8,128)(2,1)}, u32[]{:S(2)}) copy-start(bf16[512,768]{1,0:T(8,128)(2,1)} %constant.4.clone.forward_ref) | copy-start | bytes 2359300
  31.2 2.2 %copy-start.5 = (f32[256,2,351]{0,1,2:T(2,128)S(1)}, f32[256,2,351]{0,1,2:T(2,128)}, u32[]{:S(2)}) copy-start(f32[256,2,351]{0,1,2:T(2,128)} %param.9) | copy-start | bytes 2156548
  31.2 3.7 %collective-permute-start.3 = (f32[512,256]{1,0:T(8,128)S(1)}, f32[512,256]{1,0:T(8,128)S(1)}, u32[]{:S(2)}, u32[]{:S(2)}) collective-permute-start(f32[512,256]{1,0:T(8,128)S(1)} %shard_map.77.own_wide_ref), channel_id=1, source_target_pairs={{0,64},{64,0},{1,65},{65,1},{2,66},{66,2},{3,67},{67,3},{4,68},{68... | collective-permute-start | bytes 1572872 | tf_op jit(solution)/shard_map/ppermute | solution.py:323
  33.3 1.6 %collective-permute-start.4 = (f32[512,128]{1,0:T(8,128)S(1)}, f32[512,128]{1,0:T(8,128)S(1)}, u32[]{:S(2)}, u32[]{:S(2)}) collective-permute-start(f32[512,128]{1,0:T(8,128)S(1)} %shard_map.78.own_narrow_ref), channel_id=1, source_target_pairs={{0,64},{64,0},{1,65},{65,1},{2,66},{66,2},{3,67},{67,3},{4,68},{68... | collective-permute-start | bytes 786440 | tf_op jit(solution)/shard_map/ppermute | solution.py:325
  33.4 1.5 %copy-start.2 = (bf16[768,512]{1,0:T(8,128)(2,1)S(1)}, bf16[768,512]{1,0:T(8,128)(2,1)}, u32[]{:S(2)}) copy-start(bf16[768,512]{1,0:T(8,128)(2,1)} %constant.5.clone.inverse_ref) | copy-start | bytes 2359300

commit v7 on v6

--- a/solution.py
+++ b/solution.py
@@ -157,7 +157,9 @@
     )(*operands)
 
 
-def lags_kernel(series_ref, forward_ref, spectrum_ref, weight_ref):
+def lags_kernel(series_ref, forward_ref, inverse_ref, spectrum_ref, weight_ref, back_ref):
+    share = back_ref.shape[1]
+    back_ref[...] = inverse_ref[:, pl.ds(pl.multiple_of(lax.axis_index("sect") * share, share), share)]
     length, pieces, lanes = series_ref.shape
     groups = weight_ref.shape[0]
     flat = series_ref.reshape(length * pieces, lanes)
@@ -180,7 +182,7 @@
     spectrum_ref[groups:, BINS:] = real_hat[:, BINS:] - imag_hat[:, :BINS]
 
 
-def lag_spectrum(correlation, forward):
+def lag_spectrum(correlation, forward, inverse, share):
     groups, _, length = correlation.shape
     tiles = groups // LANES
     series = correlation.transpose(2, 1, 0).reshape(length, 2, tiles, LANES)
@@ -190,18 +192,50 @@
         out_shape=(
             jax.ShapeDtypeStruct((2 * groups, 2 * BINS), jnp.float32),
             jax.ShapeDtypeStruct((groups, LANES), jnp.float32),
+            jax.ShapeDtypeStruct((2 * BINS, share), jnp.bfloat16),
         ),
         compiler_params=pltpu.CompilerParams(vmem_limit_bytes=GRANT),
         cost_estimate=pl.CostEstimate(flops=1 << 30, bytes_accessed=1 << 22, transcendentals=0),
         name="lag_spectrum",
-    )(series, forward)
+    )(series, forward, inverse)
+
+
+def hold_kernel(own_ref, other_ref, held_ref):
+    section = lax.axis_index("sect")
+    tiles, columns, lanes = held_ref.shape
+    lane = lax.broadcasted_iota(jnp.int32, (columns, lanes), 1)
+
+    def placed(slow, middle):
+        for tile in range(tiles):
+            start = (tile // 2) * lanes
+            held = jnp.take_along_axis(slow[:, start : start + lanes], lane // 2 + (tile % 2) * (lanes // 2), axis=1)
+            if 0 < tile < tiles - 1:
+                held += middle[:, (tile - 1) * lanes : tile * lanes]
+            held_ref[tile] = held
+
+    @pl.when(section == 0)
+    def _():
+        placed(own_ref, other_ref)
+
+    @pl.when(section == 1)
+    def _():
+        placed(other_ref, own_ref)
+
+
+def held_tiles(own, other, tiles):
+    return pl.pallas_call(
+        hold_kernel,
+        out_shape=jax.ShapeDtypeStruct((tiles, own.shape[0], LANES), jnp.float32),
+        compiler_params=pltpu.CompilerParams(vmem_limit_bytes=GRANT),
+        cost_estimate=pl.CostEstimate(flops=1 << 28, bytes_accessed=1 << 21, transcendentals=0),
+        name="held_tiles",
+    )(own, other)
 
 
 def residual_kernel(
     half,
-    own_wide_ref,
+    held_ref,
     own_narrow_ref,
-    other_wide_ref,
     other_narrow_ref,
     spectrum_ref,
     weight_ref,
@@ -216,28 +250,21 @@
     samples = forward_ref.shape[0]
     length = 2 * half + 1
     tiles = samples // LANES
-    lane = lax.broadcasted_iota(jnp.int32, (2 * groups, LANES), 1)
-
-    def placed(slow, middle, left, right):
-        for tile in range(tiles):
-            start = (tile // 2) * LANES
-            picked = slow[:, start : start + LANES].astype(jnp.float32)
-            held = jnp.take_along_axis(picked, lane // 2 + (tile % 2) * (LANES // 2), axis=1)
-            if tile == 0:
-                fast = left[...]
-            elif tile == tiles - 1:
-                fast = right[...]
-            else:
-                fast = middle[:, (tile - 1) * LANES : tile * LANES]
-            full_ref[tile] = held + fast.astype(jnp.float32)
+    last = tiles - 1
+    for tile in range(1, last):
+        full_ref[tile] = held_ref[tile]
+
+    def ended(left, right):
+        full_ref[0] = held_ref[0] + left[...]
+        full_ref[last] = held_ref[last] + right[...]
 
     @pl.when(section == 0)
     def _():
-        placed(own_wide_ref, other_wide_ref, own_narrow_ref, other_narrow_ref)
+        ended(own_narrow_ref, other_narrow_ref)
 
     @pl.when(section == 1)
     def _():
-        placed(other_wide_ref, own_wide_ref, other_narrow_ref, own_narrow_ref)
+        ended(other_narrow_ref, own_narrow_ref)
 
     first = pl.multiple_of(section * share, share)
     mine = pl.ds(first, share)
@@ -267,7 +294,7 @@
     b_real, b_imag = imag_hat[:, :BINS], imag_hat[:, BINS:]
     p_real, p_imag = spectrum_ref[0:groups, 0:BINS], spectrum_ref[0:groups, BINS:]
     q_real, q_imag = spectrum_ref[groups:, 0:BINS], spectrum_ref[groups:, BINS:]
-    back = inverse_ref[:, mine]
+    back = inverse_ref[...]
 
     def turned(low_part, high_part):
         parts = jnp.concatenate([low_part, high_part], axis=1).astype(jnp.bfloat16)
@@ -288,7 +315,7 @@
 
 
 def residual_of(pieces, spectrum, weight, forward, inverse, half, share):
-    columns = pieces[0].shape[0]
+    columns = pieces[1].shape[0]
     return pl.pallas_call(
         functools.partial(residual_kernel, half),
         out_shape=(
@@ -323,9 +350,10 @@
     other_wide = lax.ppermute(own_wide, "sect", swap)
     own_narrow = partial_products(narrow_kernel, LANES, own_rows, other_rows, mine)
     other_narrow = lax.ppermute(own_narrow, "sect", swap)
-    spectrum, weight = lag_spectrum(correlation, forward)
-    pieces = (own_wide, own_narrow, other_wide, other_narrow)
-    return residual_of(pieces, spectrum, weight, forward, inverse, half, samples // sections)
+    spectrum, weight, back = lag_spectrum(correlation, forward, inverse, samples // sections)
+    held = held_tiles(own_wide, other_wide, samples // LANES)
+    pieces = (held, own_narrow, other_narrow)
+    return residual_of(pieces, spectrum, weight, forward, back, half, samples // sections)
 
 
 def solution(mesh):

time: 37.6 us -> 38.1 us (1.013)
  blocking collectives: 26.6 us -> 0 us
  waiting for transfers between devices: 0.74 us -> 15.1 us
  starting transfers between devices: 3.72 us -> 15.5 us
  Pallas kernels: 5.48 us -> 6.44 us
    all_to_all x1 -> x0, blocking collectives: 26.6 us -> none  [local(): mine = lax.all_to_all(block, 'tmpl', 0, 0).reshape(-1, share)]
    all_to_all x0 -> x1, waiting for transfers between devices: none -> 14.6 us  [local(): mine = lax.all_to_all(block, 'tmpl', 0, 0).reshape(-1, share)]
    all_to_all x0 -> x1, starting transfers between devices: none -> 11.2 us  [local(): mine = lax.all_to_all(block, 'tmpl', 0, 0).reshape(-1, share)]
    pallas_call x1, Pallas kernels: 0.35 us -> 1.25 us  [basis_share(): pl.pallas_call(last_kernel, out_shape=jax.ShapeDtypeStruct((chips, own.sh...]
    ppermute x1, waiting for transfers between devices: 0.73 us -> 0.17 us  [local(): other_narrow = lax.ppermute(own_narrow, 'sect', swap)]
  transfers between devices with their start and end apart: 5 -> 6, of which waited for: 1 -> 4; matrix products, arithmetic and copies ran while one was open for 0% -> 0% of each run, Pallas kernels for 8% -> 8%
where the time goes in v7:
time: 38.1 us; the launch traced here: 37.8 us
  starting transfers between devices  15.5 us (41%)
  waiting for transfers between devices  15.1 us (40%)
  Pallas kernels  6.44 us (17%)
  between operations  0.73 us (2%)
    all_to_all x1, waiting for transfers between devices, local(): mine = lax.all_to_all(block, 'tmpl', 0, 0).reshape(-1, share)  14.6 us
    all_to_all x1, starting transfers between devices, local(): mine = lax.all_to_all(block, 'tmpl', 0, 0).reshape(-1, share)  11.2 us
    pallas_call x1, Pallas kernels, residual_of(): pl.pallas_call(functools.partial(residual_kernel, half), out_shape=(jax.S...  2.09 us
    ppermute x1, starting transfers between devices, local(): other_wide = lax.ppermute(own_wide, 'sect', swap)  1.89 us
    ppermute x1, starting transfers between devices, local(): other_line = lax.ppermute(strain, 'sect', swap)  1.46 us
    pallas_call x1, Pallas kernels, basis_share(): pl.pallas_call(last_kernel, out_shape=jax.ShapeDtypeStruct((chips, own.sh...  1.25 us
    pallas_call x1, Pallas kernels, first_columns(): pl.pallas_call(first_kernel, in_specs=[pl.BlockSpec(memory_space=pltpu.HB...  1.13 us
    pallas_call x2, Pallas kernels, partial_products(): pl.pallas_call(kernel, out_shape=jax.ShapeDtypeStruct((columns, count), j...  0.86 us
  transfers between devices with their start and end apart: 6, of which 4 were waited for; matrix products, arithmetic and copies ran while one was open for 0% of the time, Pallas kernels for 8%

profile of v7, /device:TPU:1, one launch (start us, length us, event | category | flops | bytes accessed | tf_op | source)
XLA Modules:
  0.0 37.8 jit_solution(15884727569506612044)
XLA Ops:
  0.6 1.5 %collective-permute-start = (bf16[1,1535]{1,0:T(2,128)(2,1)}, bf16[1,1535]{1,0:T(2,128)(2,1)S(1)}, u32[]{:S(2)}, u32[]{:S(2)}) collective-permute-start(bf16[1,1535]{1,0:T(2,128)(2,1)} %own_line_ref.1), channel_id=1, source_target_pairs={{0,64},{64,0},{1,65},{65,1},{2,66},{66,2},{3,67},{67,3},{4,68},{68... | collective-permute-start | bytes 9218 | tf_op jit(solution)/shard_map/ppermute | solution.py:343
  2.1 0.0 copy-start.2
  2.1 0.0 copy-start.3
  2.1 0.1 collective-permute-start.1
  2.2 1.1 %first_columns.1.first_ref = bf16[16,256]{1,0:T(8,128)(2,1)S(1)} custom-call(bf16[1,1535]{1,0:T(2,128)(2,1)} %own_line_ref.1, bf16[16,1024]{1,0:T(8,128)(2,1)} %bitcast.16), custom_call_target="tpu_custom_call" | custom-call | flops 1073741824 | bytes 4194304 | tf_op jit(solution)/shard_map/first_columns/pallas_call | solution.py:75
  3.3 0.0 copy-start
  3.4 0.0 collective-permute-done.other_line_ref
  3.4 0.1 collective-permute-done.1.other_ref
  3.5 0.0 copy-done.2
  3.5 0.0 copy-done.3
  3.5 1.3 %basis_share.1 = bf16[64,16,384]{2,1,0:T(8,128)(2,1)} custom-call(bf16[1,1535]{1,0:T(2,128)(2,1)S(1)} %copy-done.3, bf16[1,1535]{1,0:T(2,128)(2,1)S(1)} %collective-permute-done.other_line_ref, bf16[16,1024]{1,0:T(8,128)(2,1)S(1)} %bitcast.17, bf16[16,1024]{1,0:T(8,128)(2,1)S(1)} %collective-permute-done.1.other_ref, bf16[16,256]{1,0:T(8,128)(2,1)S(1)} %first_columns.1.first_ref), custom_call_target="tpu_custom_call" | custom-call | tf_op jit(solution)/shard_map/basis_share/pallas_call | solution.py:111
  4.8 11.2 %all-to-all-start = ((bf16[64,16,384]{2,1,0:T(8,128)(2,1)}), bf16[64,16,384]{2,1,0:T(8,128)(2,1)S(1)}, u32[]{:S(2)}, u32[]{:S(2)}) async-start(bf16[64,16,384]{2,1,0:T(8,128)(2,1)} %basis_share.1), calls=%async_computation | async-start | bytes 1572864 | tf_op jit(solution)/shard_map/all_to_all | solution.py:348
  16.0 0.0 copy-done
  16.0 0.6 %collective-permute-start.3 = (bf16[512,1024]{1,0:T(8,128)(2,1)S(1)}, bf16[512,1024]{1,0:T(8,128)(2,1)S(1)}, u32[]{:S(2)}, u32[]{:S(2)}) collective-permute-start(bf16[512,1024]{1,0:T(8,128)(2,1)S(1)} %bitcast.12), channel_id=1, source_target_pairs={{0,64},{64,0},{1,65},{65,1},{2,66},{66,2},{3,67},{67,3},{4,68},{68... | collective-permute-start | bytes 3145736 | tf_op jit(solution)/shard_map/ppermute | solution.py:345
  16.7 14.6 %all-to-all-done = bf16[64,16,384]{2,1,0:T(8,128)(2,1)S(1)} async-done(((bf16[64,16,384]{2,1,0:T(8,128)(2,1)}), bf16[64,16,384]{2,1,0:T(8,128)(2,1)S(1)}, u32[]{:S(2)}, u32[]{:S(2)}) %all-to-all-start) | async-done | bytes 786464 | tf_op jit(solution)/shard_map/all_to_all | solution.py:348
  31.3 0.4 %shard_map.77.own_ref = f32[512,256]{1,0:T(8,128)S(1)} custom-call(bf16[512,1024]{1,0:T(8,128)(2,1)S(1)} %bitcast.13, bf16[1024,384]{1,0:T(8,128)(2,1)S(1)} %bitcast.10), custom_call_target="tpu_custom_call" | custom-call | flops 536870912 | bytes 2097152 | tf_op jit(solution)/shard_map/pallas_call | solution.py:152
  31.7 0.0 copy-start.1
  31.8 0.0 copy-start.4
  31.8 0.0 copy-start.5
  31.8 1.9 %collective-permute-start.2 = (f32[512,256]{1,0:T(8,128)S(1)}, f32[512,256]{1,0:T(8,128)S(1)}, u32[]{:S(2)}, u32[]{:S(2)}) collective-permute-start(f32[512,256]{1,0:T(8,128)S(1)} %shard_map.77.own_ref), channel_id=1, source_target_pairs={{0,64},{64,0},{1,65},{65,1},{2,66},{66,2},{3,67},{67,3},{4,68},{68... | collective-permute-start | bytes 1572872 | tf_op jit(solution)/shard_map/ppermute | solution.py:350
  33.7 0.0 collective-permute-done.3.other_ref
  33.7 0.4 %shard_map.78.own_narrow_ref = f32[512,128]{1,0:T(8,128)S(1)} custom-call(bf16[512,1024]{1,0:T(8,128)(2,1)S(1)} %bitcast.14, bf16[512,1024]{1,0:T(8,128)(2,1)S(1)} %collective-permute-done.3.other_ref, bf16[1024,384]{1,0:T(8,128)(2,1)S(1)} %bitcast.11), custom_call_target="tpu_custom_call" | custom-call | flops 536870912 | bytes 2097152 | tf_op jit(solution)/shard_map/pallas_call | solution.py:152
  34.1 0.1 collective-permute-start.4
  34.2 0.0 copy-done.1
  34.2 0.0 copy-done.4
  34.2 0.0 copy-done.5
  34.2 0.8 %lag_spectrum.1 = (f32[512,768]{1,0:T(8,128)S(1)}, f32[256,128]{1,0:T(8,128)S(1)}, bf16[768,256]{1,0:T(8,128)(2,1)S(1)}) custom-call(f32[351,4,128]{2,1,0:T(4,128)S(1)} %bitcast.18, bf16[512,768]{1,0:T(8,128)(2,1)S(1)} %copy-done.1, bf16[768,512]{1,0:T(8,128)(2,1)S(1)} %copy-done.5), custom_call_target="tpu_custom_call" | custom-call | flops 1073741824 | bytes 4194304 | tf_op jit(solution)/shard_map/lag_spectrum/pallas_call | solution.py:190
  35.0 0.2 collective-permute-done.2.other_ref
  35.2 0.3 held_tiles.1.held_ref
  35.5 0.2 collective-permute-done.4.other_narrow_ref
  35.7 2.1 %residual.1 = (bf16[512,256]{1,0:T(8,128)(2,1)}, f32[256,256]{1,0:T(8,128)}) custom-call(f32[4,512,128]{2,1,0:T(8,128)S(1)} %held_tiles.1.held_ref, f32[512,128]{1,0:T(8,128)S(1)} %shard_map.78.own_narrow_ref, f32[512,128]{1,0:T(8,128)S(1)} %collective-permute-done.4.other_narrow_ref, f32[512,768]{1,0:T(8,128)S(1)} %get-tuple-element.5.spectrum_ref, ...), custom_call_target="tpu_custom_call" | custom-call | tf_op jit(solution)/shard_map/residual/pallas_call | solution.py:319
Async XLA Ops:
  0.6 2.7 %collective-permute-start = (bf16[1,1535]{1,0:T(2,128)(2,1)}, bf16[1,1535]{1,0:T(2,128)(2,1)S(1)}, u32[]{:S(2)}, u32[]{:S(2)}) collective-permute-start(bf16[1,1535]{1,0:T(2,128)(2,1)} %own_line_ref.1), channel_id=1, source_target_pairs={{0,64},{64,0},{1,65},{65,1},{2,66},{66,2},{3,67},{67,3},{4,68},{68... | collective-permute-start | bytes 9218 | tf_op jit(solution)/shard_map/ppermute | solution.py:343
  2.1 1.4 %copy-start.2 = (bf16[1,16,1024]{2,1,0:T(8,128)(2,1)S(1)}, bf16[1,16,1024]{2,1,0:T(8,128)(2,1)}, u32[]{:S(2)}) copy-start(bf16[1,16,1024]{2,1,0:T(8,128)(2,1)} %param.7) | copy-start | bytes 98308
  2.1 1.4 %copy-start.3 = (bf16[1,1535]{1,0:T(2,128)(2,1)S(1)}, bf16[1,1535]{1,0:T(2,128)(2,1)}, u32[]{:S(2)}) copy-start(bf16[1,1535]{1,0:T(2,128)(2,1)} %own_line_ref.1) | copy-start | bytes 9214
  2.1 1.4 %collective-permute-start.1 = (bf16[16,1024]{1,0:T(8,128)(2,1)}, bf16[16,1024]{1,0:T(8,128)(2,1)S(1)}, u32[]{:S(2)}, u32[]{:S(2)}) collective-permute-start(bf16[16,1024]{1,0:T(8,128)(2,1)} %bitcast.15), channel_id=1, source_target_pairs={{0,64},{64,0},{1,65},{65,1},{2,66},{66,2},{3,67},{67,3},{4,68},{68... | collective-permute-start | bytes 98312 | tf_op jit(solution)/shard_map/ppermute | solution.py:344
  3.3 12.7 %copy-start = (bf16[1,512,1024]{2,1,0:T(8,128)(2,1)S(1)}, bf16[1,512,1024]{2,1,0:T(8,128)(2,1)}, u32[]{:S(2)}) copy-start(bf16[1,512,1024]{2,1,0:T(8,128)(2,1)} %param.8) | copy-start | bytes 3145732
  4.8 26.5 %all-to-all-start = ((bf16[64,16,384]{2,1,0:T(8,128)(2,1)}), bf16[64,16,384]{2,1,0:T(8,128)(2,1)S(1)}, u32[]{:S(2)}, u32[]{:S(2)}) async-start(bf16[64,16,384]{2,1,0:T(8,128)(2,1)} %basis_share.1), calls=%async_computation | async-start | bytes 1572864 | tf_op jit(solution)/shard_map/all_to_all | solution.py:348
  16.0 17.6 %collective-permute-start.3 = (bf16[512,1024]{1,0:T(8,128)(2,1)S(1)}, bf16[512,1024]{1,0:T(8,128)(2,1)S(1)}, u32[]{:S(2)}, u32[]{:S(2)}) collective-permute-start(bf16[512,1024]{1,0:T(8,128)(2,1)S(1)} %bitcast.12), channel_id=1, source_target_pairs={{0,64},{64,0},{1,65},{65,1},{2,66},{66,2},{3,67},{67,3},{4,68},{68... | collective-permute-start | bytes 3145736 | tf_op jit(solution)/shard_map/ppermute | solution.py:345
  31.7 2.5 %copy-start.1 = (bf16[512,768]{1,0:T(8,128)(2,1)S(1)}, bf16[512,768]{1,0:T(8,128)(2,1)}, u32[]{:S(2)}) copy-start(bf16[512,768]{1,0:T(8,128)(2,1)} %constant.4.clone.forward_ref) | copy-start | bytes 2359300
  31.8 2.5 %copy-start.4 = (f32[256,2,351]{0,1,2:T(2,128)S(1)}, f32[256,2,351]{0,1,2:T(2,128)}, u32[]{:S(2)}) copy-start(f32[256,2,351]{0,1,2:T(2,128)} %param.9) | copy-start | bytes 2156548
  31.8 2.5 %copy-start.5 = (bf16[768,512]{1,0:T(8,128)(2,1)S(1)}, bf16[768,512]{1,0:T(8,128)(2,1)}, u32[]{:S(2)}) copy-start(bf16[768,512]{1,0:T(8,128)(2,1)} %constant.5.clone.inverse_ref) | copy-start | bytes 2359300
  31.8 3.4 %collective-permute-start.2 = (f32[512,256]{1,0:T(8,128)S(1)}, f32[512,256]{1,0:T(8,128)S(1)}, u32[]{:S(2)}, u32[]{:S(2)}) collective-permute-start(f32[512,256]{1,0:T(8,128)S(1)} %shard_map.77.own_ref), channel_id=1, source_target_pairs={{0,64},{64,0},{1,65},{65,1},{2,66},{66,2},{3,67},{67,3},{4,68},{68... | collective-permute-start | bytes 1572872 | tf_op jit(solution)/shard_map/ppermute | solution.py:350
  34.1 1.6 %collective-permute-start.4 = (f32[512,128]{1,0:T(8,128)S(1)}, f32[512,128]{1,0:T(8,128)S(1)}, u32[]{:S(2)}, u32[]{:S(2)}) collective-permute-start(f32[512,128]{1,0:T(8,128)S(1)} %shard_map.78.own_narrow_ref), channel_id=1, source_target_pairs={{0,64},{64,0},{1,65},{65,1},{2,66},{66,2},{3,67},{67,3},{4,68},{68... | collective-permute-start | bytes 786440 | tf_op jit(solution)/shard_map/ppermute | solution.py:352
